TPU v7x, 32 devices: a whole 2x2x4 slice. The times are simulated.
32 devices in a mesh: wrap: 8 (over z, y), samp: 4 (over x, core).
Axes of the slice: x: 2, y: 2, z: 4, core: 2. Of those that a mesh axis runs over, the one named last changes fastest.
Arguments:
- inputs: bfloat16 [4, 64, 64, 256], P('samp', None, 'wrap'), may hold values from -6 to 6
- cotangent: bfloat16 [4, 64, 64, 256], P('samp', None, 'wrap'), may hold values from -6 to 6
- weight_one: bfloat16 [64, 1728], replicated, may hold values from -0.15625 to 0.15625
- bias_one: float32 [64], replicated, may hold values from -3 to 3
- weight_two: bfloat16 [64, 1728], replicated, may hold values from -0.15625 to 0.15625
- bias_two: float32 [64], replicated, may hold values from -3 to 3
- dilation: int32 [2], replicated, may hold values from 1 to 4, as said below
Outputs:
- prediction: bfloat16 [4, 64, 64, 256], P('samp', None, 'wrap')
- grad_weight_one: float32 [64, 1728], replicated
- grad_bias_one: float32 [64], replicated
- grad_weight_two: float32 [64, 1728], replicated
- grad_bias_two: float32 [64], replicated
Inputs may be any that keep to these rules, and one draw needn't show every extreme that they name: `dilation`: in every draw one of the two rates equals 4.
All inputs are finite; a program needn't handle non-finite values.
Results may differ from a plain program's by a relative error of at most 0.006.
Values may be sent and summed in bfloat16 or wider, within the bound.
No kernel may reach another device: no remote copies, remote signals or barrier semaphores. Data moves between devices by JAX's collectives and lax.ppermute only.
A program may use at most 128 MiB of HBM per device.

v0:
```python
import math

import jax
import jax.numpy as jnp
from jax import lax
from jax.sharding import PartitionSpec as P

DMAX = 4
NR = 16
S = 16


def with_halo(x, sides, width):
    for axis, dim in sides:
        size, length = (lax.axis_size(axis), x.shape[dim])
        up = [(i, (i + 1) % size) for i in range(size)]
        down = [(j, i) for i, j in up]
        last = lax.slice_in_dim(x, length - width, length, axis=dim)
        initial = lax.slice_in_dim(x, 0, width, axis=dim)
        before = lax.ppermute(last, axis, up)
        after = lax.ppermute(initial, axis, down)
        x = jnp.concatenate([before, x, after], axis=dim)
    return x


def grid_of(field):
    chans = field.shape[0]
    shaped = field.reshape(chans, field.shape[1], NR, S)
    return jnp.pad(shaped, ((0, 0), (0, 0), (DMAX, DMAX), (DMAX, DMAX)))


def tap_stack(padded, rate, first_row, out_rows, tap_w):
    in_chan = padded.shape[0]
    anchor = jnp.zeros((), jnp.int32)
    windows = []
    for tap_n in range(3):
        for tap_s in range(3):
            offsets = (
                anchor,
                first_row + (tap_w - 1) * rate,
                DMAX + (tap_n - 1) * rate,
                DMAX + (tap_s - 1) * rate,
            )
            window = lax.dynamic_slice(padded, offsets, (in_chan, out_rows, NR, S))
            windows.append(window.reshape(in_chan, -1))
    return jnp.concatenate(windows, 0)


def convolve(padded, weight, rate, first_row, out_rows):
    in_chan = padded.shape[0]
    summed = None
    for tap_w in range(3):
        stacked = tap_stack(padded, rate, first_row, out_rows, tap_w)
        term = jnp.dot(
            weight[:, tap_w * 9 * in_chan : (tap_w + 1) * 9 * in_chan],
            stacked,
            preferred_element_type=jnp.float32,
        )
        summed = term if summed is None else summed + term
    return summed


def weight_grad(cot, padded, rate, first_row, out_rows):
    columns = []
    for tap_w in range(3):
        stacked = tap_stack(padded, rate, first_row, out_rows, tap_w)
        columns.append(
            lax.dot_general(
                cot, stacked, (((1,), (1,)), ((), ())), preferred_element_type=jnp.float32
            )
        )
    return jnp.concatenate(columns, 1)


def flip_kernel(weight):
    chans = weight.shape[0]
    shaped = weight.reshape(chans, 27, chans)[:, ::-1, :]
    return jnp.transpose(shaped, (2, 1, 0)).reshape(chans, 27 * chans)


def body(inputs, cotangent, weight_one, bias_one, weight_two, bias_two, dilation):
    samples_here = inputs.shape[0]
    chans = inputs.shape[1]
    rows = inputs.shape[2]
    first_rate = dilation[0]
    second_rate = dilation[1]
    factor = 1.0 / math.sqrt(
        samples_here * lax.axis_size("samp") * rows * lax.axis_size("wrap") * inputs.shape[3]
    )
    flipped = flip_kernel(weight_two)
    extended = with_halo(inputs, (("wrap", 2),), DMAX)
    sample = 0
    grid_in = grid_of(extended[sample])
    pre_one = convolve(grid_in, weight_one, first_rate, DMAX, rows) + bias_one[:, None]
    pre_list = [pre_one]
    hidden_list = [jax.nn.silu(pre_one).astype(jnp.bfloat16).reshape(chans, rows, -1)]
    grids = [grid_in]
    hidden_ext = with_halo(jnp.stack(hidden_list), (("wrap", 2),), DMAX)
    sample = 0
    hidden_grids = [grid_of(hidden_ext[sample])]
    input_first = DMAX
    grad_two = None
    bias_two_grad = None
    sample = 0
    output = (
        convolve(hidden_grids[sample], weight_two, second_rate, DMAX, rows) + bias_two[:, None]
    ).astype(jnp.bfloat16)
    outputs = [output.reshape(chans, rows, -1)]
    cot_flat = cotangent[sample].reshape(chans, -1)
    term = weight_grad(cot_flat, hidden_grids[sample], second_rate, DMAX, rows)
    bias_term = jnp.sum(cot_flat.astype(jnp.float32), 1)
    grad_two = term
    bias_two_grad = bias_term
    grad_two = grad_two * factor
    bias_two_grad = bias_two_grad * factor
    cot_ext = with_halo(cotangent, (("wrap", 2),), DMAX)
    grad_one = None
    bias_one_grad = None
    sample = 0
    back_hidden = convolve(grid_of(cot_ext[sample]), flipped, second_rate, DMAX, rows)
    pre_one = pre_list[sample]
    sigm = jax.nn.sigmoid(pre_one)
    back_pre = (back_hidden * sigm * (1.0 + pre_one * (1.0 - sigm))).astype(jnp.bfloat16)
    term = weight_grad(back_pre, grids[sample], first_rate, input_first, rows)
    bias_term = jnp.sum(back_pre.astype(jnp.float32), 1)
    grad_one = term
    bias_one_grad = bias_term
    grad_one = grad_one * factor
    bias_one_grad = bias_one_grad * factor
    grad_one, bias_one_grad, grad_two, bias_two_grad = lax.psum(
        (grad_one, bias_one_grad, grad_two, bias_two_grad), ("wrap", "samp")
    )
    return (jnp.stack(outputs), grad_one, bias_one_grad, grad_two, bias_two_grad)


def solution(mesh):
    in_specs = (
        P("samp", None, "wrap", None),
        P("samp", None, "wrap", None),
        P(),
        P(),
        P(),
        P(),
        P(),
    )
    out_specs = (P("samp", None, "wrap", None), P(), P(), P(), P())
    return jax.shard_map(body, mesh=mesh, in_specs=in_specs, out_specs=out_specs, check_vma=False)
```

profile of v0, /device:TPU:0, one launch (start us, length us, event | category | flops | bytes accessed | tf_op | source)
XLA Modules:
  0.0 347.6 jit_solution(2324225012075709310)
XLA Ops:
  7.2 1.3 copy.26
  8.6 0.7 fusion.28
  9.3 3.0 collective-permute-start.4
  12.3 3.0 collective-permute-start.5
  15.4 1.3 copy.12
  16.8 4.7 %collective-permute-start.1 = (bf16[1,64,4,256]{1,3,2,0:T(8,128)(2,1)S(1)}, bf16[1,64,4,256]{1,3,2,0:T(8,128)(2,1)}, u32[]{:S(2)}, u32[]{:S(2)}) collective-permute-start(bf16[1,64,4,256]{1,3,2,0:T(8,128)(2,1)S(1)} %get-tuple-element.94), channel_id=1, source_target_pairs={{4,0},{8,4},{12,8},{16,12},{20,16},{24,20},{28,24},{0,28},{5,1},{9... | collective-permute-start | bytes 393224 | tf_op jit(solution)/shard_map/ppermute | solution.py:21
  21.5 0.6 fusion.31
  27.2 0.6 convert_reduce_fusion
  28.8 1.1 copy.29
  29.9 1.1 reshape.409
  31.1 1.7 collective-permute-done.5
  32.8 1.3 pad_maximum_fusion.1
  34.1 4.6 %pad_dynamic-slice_fusion = (bf16[64,8,16,16]{0,3,2,1:T(8,128)(2,1)}, bf16[64,8,16,16]{0,3,2,1:T(8,128)(2,1)}, bf16[64,8,16,16]{0,3,2,1:T(8,128)(2,1)}, bf16[64,...) fusion(s32[]{:T(128)S(6)} %select_n.23, ...), kind=kLoop, calls=%fused_computation | loop fusion | bytes 5505040 | tf_op jit(solution)/shard_map/dynamic_slice | solution.py:44
  38.7 4.6 %pad_dynamic-slice_fusion.1 = (bf16[64,8,16,16]{0,3,2,1:T(8,128)(2,1)}, bf16[64,8,16,16]{0,3,2,1:T(8,128)(2,1)}, bf16[64,8,16,16]{0,3,2,1:T(8,128)(2,1)}, bf16[6...) fusion(s32[]{:T(128)S(6)} %select_n.23, ...), kind=kLoop, calls=%fused_computation.1 | loop fusion | bytes 3670032 | tf_op jit(solution)/shard_map/dynamic_slice | solution.py:44
  43.4 1.3 pad_maximum_fusion
  44.6 4.6 %pad_dynamic-slice_fusion.26 = (bf16[64,8,16,16]{0,3,2,1:T(8,128)(2,1)}, bf16[64,8,16,16]{0,3,2,1:T(8,128)(2,1)}, bf16[64,8,16,16]{0,3,2,1:T(8,128)(2,1)}, bf16[...) fusion(s32[]{:T(128)S(6)} %select_n.19, ...), kind=kLoop, calls=%fused_computation.26 | loop fusion | bytes 5505040 | tf_op jit(solution)/shard_map/dynamic_slice | solution.py:44
  49.2 4.5 %pad_dynamic-slice_fusion.27 = (bf16[64,8,16,16]{0,3,2,1:T(8,128)(2,1)}, bf16[64,8,16,16]{0,3,2,1:T(8,128)(2,1)}, bf16[64,8,16,16]{0,3,2,1:T(8,128)(2,1)}, bf16[...) fusion(s32[]{:T(128)S(6)} %select_n.19, ...), kind=kLoop, calls=%fused_computation.27 | loop fusion | bytes 3670032 | tf_op jit(solution)/shard_map/dynamic_slice | solution.py:44
  53.8 5.2 %concatenate.67 = bf16[576,2048]{0,1:T(8,128)(2,1)S(1)} concatenate(bf16[64,2048]{0,1:T(8,128)(2,1)} %bitcast.166, bf16[64,2048]{0,1:T(8,128)(2,1)S(1)} %bitcast.163, bf16[64,2048]{0,1:T(8,128)(2,1)} %bitcast.212, bf16[64,2048]{0,1:T(8,128)(2,1)} %bitcast.164, bf16[64,2048]{0,1:T(8,128)(2,1)} %bitcast.165, bf16[64,2048]{0,1:T(8,128)(2,1)} %bitcast.211, ...), dimensions={0} | concatenate | bytes 4718592 | tf_op jit(solution)/shard_map/concatenate | solution.py:46
  59.0 1.8 fusion.17
  60.8 5.5 %concatenate.68 = bf16[576,2048]{0,1:T(8,128)(2,1)S(1)} concatenate(bf16[64,2048]{0,1:T(8,128)(2,1)} %bitcast.154, bf16[64,2048]{0,1:T(8,128)(2,1)} %bitcast.155, bf16[64,2048]{0,1:T(8,128)(2,1)} %bitcast.162, bf16[64,2048]{0,1:T(8,128)(2,1)} %bitcast.156, bf16[64,2048]{0,1:T(8,128)(2,1)} %bitcast.157, bf16[64,2048]{0,1:T(8,128)(2,1)} %bitcast.161, bf16[64,2048]{0,1:T(8,128)(2,1)} %bitcast.160, ...), dimensions={0} | concatenate | bytes 4718592 | tf_op jit(solution)/shard_map/concatenate | solution.py:46
  66.3 2.6 convolution_add_fusion.2
  69.0 5.3 %concatenate.56 = bf16[576,2048]{0,1:T(8,128)(2,1)S(1)} concatenate(bf16[64,2048]{0,1:T(8,128)(2,1)} %bitcast.190, bf16[64,2048]{0,1:T(8,128)(2,1)} %bitcast.187, bf16[64,2048]{0,1:T(8,128)(2,1)} %bitcast.224, bf16[64,2048]{0,1:T(8,128)(2,1)} %bitcast.188, bf16[64,2048]{0,1:T(8,128)(2,1)} %bitcast.189, bf16[64,2048]{0,1:T(8,128)(2,1)} %bitcast.223, bf16[64,2048]{0,1:T(8,128)(2,1)} %bitcast.222, ...), dimensions={0} | concatenate | bytes 4718592 | tf_op jit(solution)/shard_map/concatenate | solution.py:46
  74.3 1.8 fusion.26
  76.1 6.8 %concatenate.57 = bf16[576,2048]{0,1:T(8,128)(2,1)} concatenate(bf16[64,2048]{0,1:T(8,128)(2,1)} %bitcast.178, bf16[64,2048]{0,1:T(8,128)(2,1)} %bitcast.179, bf16[64,2048]{0,1:T(8,128)(2,1)} %bitcast.186, bf16[64,2048]{0,1:T(8,128)(2,1)} %bitcast.180, bf16[64,2048]{0,1:T(8,128)(2,1)} %bitcast.181, bf16[64,2048]{0,1:T(8,128)(2,1)} %bitcast.185, bf16[64,2048]{0,1:T(8,128)(2,1)} %bitcast.184, ...), dimensions={0} | concatenate | bytes 4718592 | tf_op jit(solution)/shard_map/concatenate | solution.py:46
  82.9 3.5 %convolution_add_fusion.4 = f32[2048,64]{0,1:T(8,128)} fusion(f32[2048,64]{0,1:T(8,128)S(1)} %fusion.26, bf16[576,2048]{0,1:T(8,128)(2,1)} %concatenate.57, bf16[64,1728]{1,0:T(8,128)(2,1)} %param.9), kind=kOutput, calls=%fused_computation.75 | convolution fusion | flops 151126016 | bytes 3751936 | tf_op jit(solution)/shard_map/dot_general | solution.py:54
  86.4 6.8 %concatenate.58 = bf16[576,2048]{0,1:T(8,128)(2,1)} concatenate(bf16[64,2048]{0,1:T(8,128)(2,1)} %bitcast.220, bf16[64,2048]{0,1:T(8,128)(2,1)} %bitcast.219, bf16[64,2048]{0,1:T(8,128)(2,1)} %bitcast.218, bf16[64,2048]{0,1:T(8,128)(2,1)} %bitcast.217, bf16[64,2048]{0,1:T(8,128)(2,1)} %bitcast.216, bf16[64,2048]{0,1:T(8,128)(2,1)} %bitcast.215, bf16[64,2048]{0,1:T(8,128)(2,1)} %bitcast.214, ...), dimensions={0} | concatenate | bytes 4718592 | tf_op jit(solution)/shard_map/concatenate | solution.py:46
  93.3 3.7 %multiply_convert_fusion = (bf16[64,2048]{1,0:T(8,128)(2,1)}, f32[64,2048]{1,0:T(8,128)}) fusion(f32[64]{0:T(128)S(1)} %copy-done.17, f32[2048,64]{0,1:T(8,128)} %convolution_add_fusion.4, bf16[576,2048]{0,1:T(8,128)(2,1)} %concatenate.58, bf16[64,1728]{1,0:T(8,128)(2,1)} %param.9), kind=kOutput, calls=%fused_computation.85 | convolution fusion | flops 151912448 | bytes 4014336 | tf_op jit(solution)/shard_map/dot_general | solution.py:54
  97.0 6.7 %concatenate.69 = bf16[576,2048]{0,1:T(8,128)(2,1)} concatenate(bf16[64,2048]{0,1:T(8,128)(2,1)} %bitcast.208, bf16[64,2048]{0,1:T(8,128)(2,1)} %bitcast.207, bf16[64,2048]{0,1:T(8,128)(2,1)} %bitcast.206, bf16[64,2048]{0,1:T(8,128)(2,1)} %bitcast.205, bf16[64,2048]{0,1:T(8,128)(2,1)} %bitcast.204, bf16[64,2048]{0,1:T(8,128)(2,1)} %bitcast.203, bf16[64,2048]{0,1:T(8,128)(2,1)} %bitcast.202, ...), dimensions={0} | concatenate | bytes 4718592 | tf_op jit(solution)/shard_map/concatenate | solution.py:46
  103.7 3.2 convert_reduce_fusion.1
  106.9 0.5 fusion.34
  107.5 1.2 copy-done
  108.6 1.2 fusion.33
  109.9 1.2 fusion.32
  111.7 4.5 %collective-permute-start.3 = (bf16[1,64,4,256]{1,3,2,0:T(8,128)(2,1)S(1)}, bf16[1,64,4,256]{1,3,2,0:T(8,128)(2,1)S(1)}, u32[]{:S(2)}, u32[]{:S(2)}) collective-permute-start(bf16[1,64,4,256]{1,3,2,0:T(8,128)(2,1)S(1)} %get-tuple-element.92), channel_id=1, source_target_pairs={{4,0},{8,4},{12,8},{16,12},{20,16},{24,20},{28,24},{0,28},{5,1},{9... | collective-permute-start | bytes 393224 | tf_op jit(solution)/shard_map/ppermute | solution.py:21
  116.2 1.9 concatenate.70
  118.0 40.3 %all-reduce.3 = (f32[64]{0:T(128)}, f32[64]{0:T(128)}) all-reduce(f32[64]{0:T(128)S(1)} %broadcast_multiply_fusion.3, f32[64]{0:T(128)S(1)} %broadcast_multiply_fusion.2), channel_id=1, replica_groups=mesh['wrap'=8,'samp'=4] {'wrap','samp'}, use_global_device_ids=true, to_apply=%region_2.3 | all-reduce | flops 128 | bytes 1024 | tf_op jit(solution)/shard_map/psum | solution.py:130
  158.4 2.6 select_maximum_fusion
  161.0 7.1 %constant_dynamic-slice_fusion.9 = (bf16[64,8,16,16]{0,3,2,1:T(8,128)(2,1)S(1)}, bf16[64,8,16,16]{0,3,2,1:T(8,128)(2,1)}, bf16[64,8,16,16]{0,3,2,1:T(8,128)(2,1)...) fusion(bf16[64,16,24,24]{0,3,2,1:T(8,128)(2,1)S(1)} %select_max, ...), kind=kLoop, calls=%fused_computation.120 | loop fusion | bytes 13631504 | tf_op jit(solution)/shard_map/dynamic_slice | solution.py:44
  168.1 0.9 copy.18
  169.0 1.0 constant_dynamic-update-slice_fusion.8
  170.0 1.9 copy.19
  171.9 1.9 copy.20
  173.9 2.0 copy.21
  175.8 1.0 constant_dynamic-update-slice_fusion.7
  176.8 1.0 constant_dynamic-update-slice_fusion.6
  177.8 1.0 constant_dynamic-update-slice_fusion.5
  178.8 2.3 copy.22
  181.1 1.9 copy.23
  183.0 1.9 copy.24
  185.0 0.9 copy.25
  185.9 5.3 %concatenate.63 = bf16[576,2048]{0,1:T(8,128)(2,1)S(1)} concatenate(bf16[64,2048]{0,1:T(8,128)(2,1)} %bitcast.200, bf16[64,2048]{0,1:T(8,128)(2,1)} %bitcast.199, bf16[64,2048]{0,1:T(8,128)(2,1)} %bitcast.198, bf16[64,2048]{0,1:T(8,128)(2,1)} %bitcast.197, bf16[64,2048]{0,1:T(8,128)(2,1)} %bitcast.196, bf16[64,2048]{0,1:T(8,128)(2,1)} %bitcast.195, bf16[64,2048]{0,1:T(8,128)(2,1)} %bitcast.194, ...), dimensions={0} | concatenate | bytes 4718592 | tf_op jit(solution)/shard_map/concatenate | solution.py:46
  191.2 1.8 fusion.22
  193.1 1.2 convolution_bitcast_fusion.1
  195.0 1.5 convolution_bitcast_fusion.2
  196.5 5.3 %concatenate.65 = bf16[576,2048]{0,1:T(8,128)(2,1)S(1)} concatenate(bf16[64,2048]{0,1:T(8,128)(2,1)} %bitcast.175, bf16[64,2048]{0,1:T(8,128)(2,1)} %bitcast.174, bf16[64,2048]{0,1:T(8,128)(2,1)} %bitcast.173, bf16[64,2048]{0,1:T(8,128)(2,1)} %bitcast.172, bf16[64,2048]{0,1:T(8,128)(2,1)} %bitcast.171, bf16[64,2048]{0,1:T(8,128)(2,1)} %bitcast.170, bf16[64,2048]{0,1:T(8,128)(2,1)} %bitcast.169, ...), dimensions={0} | concatenate | bytes 4718592 | tf_op jit(solution)/shard_map/concatenate | solution.py:46
  201.8 1.2 convolution_bitcast_fusion
  203.0 2.0 concatenate.71
  205.0 2.1 broadcast_multiply_fusion
  207.2 2.0 fusion.19
  209.1 1.5 fusion.13
  210.7 0.8 copy.31
  211.4 125.7 %all-reduce.7.cloned.1.call-done = (f32[64,1728]{1,0:T(8,128)}, f32[64,1728]{1,0:T(8,128)}) async-done(((f32[64,1728]{1,0:T(8,128)}, f32[64,1728]{1,0:T(8,128)}), (f32[64,1728]{1,0:T(8,128)}, f32[64,1728]{1,0:T(8,128)})) %all-reduce.7.cloned.1.call-update) | async-done | bytes 884752 | tf_op jit(solution)/shard_map/psum | solution.py:130
  337.1 1.8 copy.43
  338.9 1.8 copy.44
  (57 shorter events, 2.5 us)
Async XLA Ops:
  7.2 20.1 %copy-start.6 = (bf16[1,64,8,256]{3,2,1,0:T(8,128)(2,1)S(1)}, bf16[1,64,8,256]{3,2,1,0:T(8,128)(2,1)}, u32[]{:S(2)}) copy-start(bf16[1,64,8,256]{3,2,1,0:T(8,128)(2,1)} %param.8) | copy-start | bytes 786436
  7.2 14.3 %copy-start.15 = (s32[2]{0:T(128)S(1)}, s32[2]{0:T(128)}, u32[]{:S(2)}) copy-start(s32[2]{0:T(128)} %param.13) | copy-start | bytes 28
  7.2 20.6 %copy-start.14 = (bf16[64,1728]{1,0:T(8,128)(2,1)S(1)}, bf16[64,1728]{1,0:T(8,128)(2,1)}, u32[]{:S(2)}) copy-start(bf16[64,1728]{1,0:T(8,128)(2,1)} %param.11) | copy-start | bytes 663556
  7.2 329.9 %all-reduce.7.cloned.1.call-start = ((), (), s32[]{:S(2)}) async-start(), calls=%async_computation | async-start | bytes 1835008 | tf_op jit(solution)/shard_map/psum | solution.py:130
  9.3 21.8 %collective-permute-start.4 = (bf16[1,64,4,256]{1,3,2,0:T(8,128)(2,1)}, bf16[1,64,4,256]{1,3,2,0:T(8,128)(2,1)}, u32[]{:S(2)}, u32[]{:S(2)}) collective-permute-start(bf16[1,64,4,256]{1,3,2,0:T(8,128)(2,1)} %get-tuple-element.89), channel_id=1, source_target_pairs={{0,4},{4,8},{8,12},{12,16},{16,20},{20,24},{24,28},{28,0},{1,5},{5... | collective-permute-start | bytes 393224 | tf_op jit(solution)/shard_map/ppermute | solution.py:20
  12.3 20.5 %collective-permute-start.5 = (bf16[1,64,4,256]{1,3,2,0:T(8,128)(2,1)S(1)}, bf16[1,64,4,256]{1,3,2,0:T(8,128)(2,1)}, u32[]{:S(2)}, u32[]{:S(2)}) collective-permute-start(bf16[1,64,4,256]{1,3,2,0:T(8,128)(2,1)S(1)} %get-tuple-element.90), channel_id=1, source_target_pairs={{4,0},{8,4},{12,8},{16,12},{20,16},{24,20},{28,24},{0,28},{5,1},{9... | collective-permute-start | bytes 393224 | tf_op jit(solution)/shard_map/ppermute | solution.py:21
  16.7 26.7 %collective-permute-start = (bf16[1,64,4,256]{1,3,2,0:T(8,128)(2,1)S(1)}, bf16[1,64,4,256]{1,3,2,0:T(8,128)(2,1)}, u32[]{:S(2)}, u32[]{:S(2)}) collective-permute-start(bf16[1,64,4,256]{1,3,2,0:T(8,128)(2,1)S(1)} %get-tuple-element.93), channel_id=1, source_target_pairs={{0,4},{4,8},{8,12},{12,16},{16,20},{20,24},{24,28},{28,0},{1,5},{5... | collective-permute-start | bytes 393224 | tf_op jit(solution)/shard_map/ppermute | solution.py:20
  16.8 26.6 %collective-permute-start.1 = (bf16[1,64,4,256]{1,3,2,0:T(8,128)(2,1)S(1)}, bf16[1,64,4,256]{1,3,2,0:T(8,128)(2,1)}, u32[]{:S(2)}, u32[]{:S(2)}) collective-permute-start(bf16[1,64,4,256]{1,3,2,0:T(8,128)(2,1)S(1)} %get-tuple-element.94), channel_id=1, source_target_pairs={{4,0},{8,4},{12,8},{16,12},{20,16},{24,20},{28,24},{0,28},{5,1},{9... | collective-permute-start | bytes 393224 | tf_op jit(solution)/shard_map/ppermute | solution.py:21
  49.2 4.5 %copy-start.8 = (bf16[64,8,16,16]{0,3,2,1:T(8,128)(2,1)S(1)}, bf16[64,8,16,16]{0,3,2,1:T(8,128)(2,1)}, u32[]{:S(2)}) copy-start(bf16[64,8,16,16]{0,3,2,1:T(8,128)(2,1)} %get-tuple-element.36) | copy-start | bytes 786436
  86.4 6.8 %copy-start.17 = (f32[64]{0:T(128)S(1)}, f32[64]{0:T(128)}, u32[]{:S(2)}) copy-start(f32[64]{0:T(128)} %param.10) | copy-start | bytes 772
  93.2 3.8 %copy-start.7 = (bf16[64,8,16,16]{0,3,2,1:T(8,128)(2,1)S(1)}, bf16[64,8,16,16]{0,3,2,1:T(8,128)(2,1)}, u32[]{:S(2)}) copy-start(bf16[64,8,16,16]{0,3,2,1:T(8,128)(2,1)} %get-tuple-element.35) | copy-start | bytes 786436
  103.7 3.2 copy-start.5
  106.9 1.8 copy-start
  108.6 2.4 copy-start.9
  111.4 47.0 %collective-permute-start.2 = (bf16[1,64,4,256]{1,3,2,0:T(8,128)(2,1)S(1)}, bf16[1,64,4,256]{1,3,2,0:T(8,128)(2,1)S(1)}, u32[]{:S(2)}, u32[]{:S(2)}) collective-permute-start(bf16[1,64,4,256]{1,3,2,0:T(8,128)(2,1)S(1)} %get-tuple-element.91), channel_id=1, source_target_pairs={{0,4},{4,8},{8,12},{12,16},{16,20},{20,24},{24,28},{28,0},{1,5},{5... | collective-permute-start | bytes 393224 | tf_op jit(solution)/shard_map/ppermute | solution.py:20
  111.7 46.7 %collective-permute-start.3 = (bf16[1,64,4,256]{1,3,2,0:T(8,128)(2,1)S(1)}, bf16[1,64,4,256]{1,3,2,0:T(8,128)(2,1)S(1)}, u32[]{:S(2)}, u32[]{:S(2)}) collective-permute-start(bf16[1,64,4,256]{1,3,2,0:T(8,128)(2,1)S(1)} %get-tuple-element.92), channel_id=1, source_target_pairs={{4,0},{8,4},{12,8},{16,12},{20,16},{24,20},{28,24},{0,28},{5,1},{9... | collective-permute-start | bytes 393224 | tf_op jit(solution)/shard_map/ppermute | solution.py:21
  178.8 7.1 %copy-start.1 = (bf16[576,2048]{1,0:T(8,128)(2,1)}, bf16[576,2048]{1,0:T(8,128)(2,1)S(1)}, u32[]{:S(2)}) copy-start(bf16[576,2048]{1,0:T(8,128)(2,1)S(1)} %constant_dynamic-update-slice_fusion.4) | copy-start | bytes 7077892
  191.2 3.1 copy-start.12
  193.1 1.7 copy-start.2
  193.1 1.7 copy-start.13
  193.1 1.8 copy-start.11
  193.1 1.8 copy-start.10
  195.0 1.5 copy-start.3
  207.1 2.0 copy-start.4
  207.2 2.0 copy-start.16
Sparse Core Ops, SparseCore 0:
  207.3 129.7 all-reduce.6
where the time goes:
time: 351 us; the launch traced here: 348 us
  waiting for transfers between devices  127 us (36%)
  local copies, waits for them, and re-layouts  108 us (31%)
  blocking collectives  40.3 us (11%)
  matrix products  28.9 us (8%)
  between operations  19.6 us (6%)
  starting transfers between devices  15.6 us (4%)
  other arithmetic  7.83 us (2%)
    psum x1, waiting for transfers between devices, body(): lax.psum((grad_one, bias_one_grad, grad_two, bias_two_grad), ('wrap', 'sa...  126 us
    concatenate x9, local copies, waits for them, and re-layouts, tap_stack(): return jnp.concatenate(windows, 0)  47 us
    psum x1, blocking collectives, body(): lax.psum((grad_one, bias_one_grad, grad_two, bias_two_grad), ('wrap', 'sa...  40.3 us
    dynamic_slice x5, local copies, waits for them, and re-layouts, tap_stack(): window = lax.dynamic_slice(padded, offsets, (in_chan, out_rows, NR, S))  25.5 us
    dot_general x9, matrix products, convolve(): jnp.dot(weight[:, tap_w * 9 * in_chan:(tap_w + 1) * 9 * in_chan], stacked...  22 us
    reshape x8, local copies, waits for them, and re-layouts, tap_stack(): windows.append(window.reshape(in_chan, -1))  13.8 us
    unnamed x50, local copies, waits for them, and re-layouts  12.8 us
    ppermute x3, starting transfers between devices, with_halo(): after = lax.ppermute(initial, axis, down)  12.3 us
  transfers between devices with their start and end apart: 7, of which 2 were waited for; matrix products, arithmetic and copies ran while one was open for 6% of the time, Pallas kernels for 0%

commit v1 on v0

v1 whole, which is shorter than its diff:
```python
import math

import jax
import jax.numpy as jnp
from jax import lax
from jax.experimental import pallas as pl
from jax.experimental.pallas import tpu as pltpu
from jax.sharding import Mesh
from jax.sharding import PartitionSpec as P

DMAX = 4
NR = 16
S = 16
NS = NR * S
CH = 64
BF = jnp.bfloat16
F32 = jnp.float32

VM = pl.BlockSpec(memory_space=pltpu.VMEM)
SM = pl.BlockSpec(memory_space=pltpu.SMEM)


def sds(shape, dtype):
    return jax.ShapeDtypeStruct(shape, dtype)


def call(kernel, outs, scratch=(), ins=None, flops=0, nbytes=0, name=None):
    return pl.pallas_call(
        kernel,
        out_shape=outs,
        in_specs=ins,
        out_specs=jax.tree.map(lambda _: VM, outs),
        scratch_shapes=list(scratch),
        cost_estimate=pl.CostEstimate(flops=flops, bytes_accessed=nbytes, transcendentals=0),
        compiler_params=pltpu.CompilerParams(vmem_limit_bytes=60 * 1024 * 1024),
        name=name,
    )


def nt(a, b):
    return lax.dot_general(a, b, (((1,), (1,)), ((), ())), preferred_element_type=F32)


def mm(a, b):
    return jnp.dot(a, b, preferred_element_type=F32)


def shift_matrix(tap, rate):
    dn = tap // 3 - 1
    ds = tap % 3 - 1
    src = lax.broadcasted_iota(jnp.int32, (NS, NS), 0)
    dst = lax.broadcasted_iota(jnp.int32, (NS, NS), 1)
    span = (dst & (S - 1)) + ds * rate
    hit = (src - dst == (dn * S + ds) * rate) & (span >= 0) & (span < S)
    return jnp.where(hit, 1.0, 0.0).astype(BF)


def swap_rows(x, major, minor):
    size = major * minor
    dst = lax.broadcasted_iota(jnp.int32, (size, size), 0)
    src = lax.broadcasted_iota(jnp.int32, (size, size), 1)
    want = (dst % major) * minor + dst // major
    perm = jnp.where(src == want, 1.0, 0.0).astype(BF)
    return mm(perm, x).astype(BF)


def shifted(x, rate, stack_ref):
    rows = x.shape[0] // CH

    def one(tap, carry):
        moved = mm(x, shift_matrix(tap, rate)).astype(BF)
        at = pl.ds(pl.multiple_of(tap * CH, CH), CH)
        for w in range(rows):
            stack_ref[at, w * NS : (w + 1) * NS] = moved[w * CH : (w + 1) * CH]
        return carry

    lax.fori_loop(0, 9, one, 0, unroll=True)


def lanes(row, count):
    return pl.ds(pl.multiple_of(row * NS, NS), count * NS)


def prep_kernel(rows, x_ref, c_ref, xp_ref, cp_ref, top_ref, bottom_ref):
    half = DMAX * CH
    for k, (src, dst) in enumerate(((x_ref, xp_ref), (c_ref, cp_ref))):
        swapped = swap_rows(src[...], CH, rows)
        dst[...] = swapped
        top_ref[k * half : (k + 1) * half] = swapped[:half]
        bottom_ref[k * half : (k + 1) * half] = swapped[rows * CH - half :]


def local_part(rows, x_ref, rate, w_ref, stack_ref, part_ref, pad_ref):
    shifted(x_ref[...], rate, stack_ref)
    pad_ref[...] = jnp.zeros_like(pad_ref)
    z = mm(w_ref[...], stack_ref[...])
    pad_ref[:, lanes(DMAX + rate, rows)] += z[:CH]
    pad_ref[:, lanes(DMAX, rows)] += z[CH : 2 * CH]
    pad_ref[:, lanes(DMAX - rate, rows)] += z[2 * CH :]
    part_ref[...] = pad_ref[:, DMAX * NS : (DMAX + rows) * NS]


def local_kernel(rows, d_ref, xp_ref, cp_ref, w1_ref, wf_ref, xs_ref, cs_ref, pre_ref, back_ref, pad_ref):
    local_part(rows, xp_ref, d_ref[0], w1_ref, xs_ref, pre_ref, pad_ref)
    local_part(rows, cp_ref, d_ref[1], wf_ref, cs_ref, back_ref, pad_ref)


def halo_part(rows, before, after, rate, w_ref, stack_ref, part, pad_ref):
    shifted(jnp.concatenate([before, after], 0), rate, stack_ref)
    pad_ref[:, DMAX * NS : (DMAX + rows) * NS] = part
    near = DMAX * NS
    pad_ref[:, lanes(rate, DMAX)] += mm(w_ref[:CH], stack_ref[:, :near])
    pad_ref[:, lanes(DMAX + rows - rate, DMAX)] += mm(w_ref[2 * CH :], stack_ref[:, near:])
    return pad_ref[:, DMAX * NS : (DMAX + rows) * NS]


def triple(rows, value, rate, pad_ref, out_ref):
    ext = rows + 2 * DMAX
    pad_ref[...] = jnp.zeros_like(pad_ref)
    pad_ref[:, 2 * DMAX * NS : (2 * DMAX + rows) * NS] = value
    for w in range(3):
        out_ref[w * CH : (w + 1) * CH] = pad_ref[:, lanes(DMAX + (1 - w) * rate, ext)]


def grad_kernel(
    rows, total, factor,
    d_ref, core_ref, b1_ref, up_ref, down_ref, w1_ref, wf_ref, xs_ref, cs_ref, pre_ref, back_ref, cp_ref,
    hid_ref, keep_ref, send_ref,
    pad_ref, pad16_ref, tri_ref, xh_ref, ch_ref, all_ref,
):
    r1 = d_ref[0]
    r2 = d_ref[1]
    half = DMAX * CH
    near = DMAX * NS
    mid = slice(near, near + rows * NS)
    far = slice(near + rows * NS, 2 * near + rows * NS)
    up = up_ref[...]
    down = down_ref[...]
    pre = halo_part(rows, up[:half], down[:half], r1, w1_ref, xh_ref, pre_ref[...], pad_ref) + b1_ref[...]
    sigm = 1.0 / (1.0 + jnp.exp(-pre))
    hidden = (pre * sigm).astype(BF)
    for w in range(rows):
        hid_ref[w * CH : (w + 1) * CH] = hidden[:, w * NS : (w + 1) * NS]
    slope = sigm * (1.0 + pre * (1.0 - sigm))
    back = halo_part(rows, up[half:], down[half:], r2, wf_ref, ch_ref, back_ref[...], pad_ref)
    back_pre = (back * slope).astype(BF)

    triple(rows, hidden, r2, pad16_ref, tri_ref)
    g2 = nt(cs_ref[...], tri_ref[:, mid])
    g2a = nt(ch_ref[:, :near], tri_ref[:CH, :near])
    g2b = nt(ch_ref[:, near:], tri_ref[2 * CH :, far])
    all_ref[:576] = jnp.concatenate([g2[:, :CH] + g2a, g2[:, CH : 2 * CH]], 1) * factor
    left2 = (g2[:, 2 * CH :] + g2b) * factor

    triple(rows, back_pre, r1, pad16_ref, tri_ref)
    g1 = nt(tri_ref[:, mid], xs_ref[...])
    g1a = nt(tri_ref[:CH, :near], xh_ref[:, :near])
    g1b = nt(tri_ref[2 * CH :, far], xh_ref[:, near:])
    g1 = jnp.concatenate([g1[:CH] + g1a, g1[CH : 2 * CH], g1[2 * CH :] + g1b], 0) * factor
    for k in range(4):
        all_ref[576 + 192 * k : 768 + 192 * k] = g1[:, 128 * k : 128 * (k + 1)]
    right = jnp.concatenate([left2[384:], g1[:, 512:]], 0)
    all_ref[1344:1728] = jnp.concatenate([left2[:384], right], 1)
    sum_one = jnp.sum(back_pre.astype(F32), 1, keepdims=True) * factor
    sum_two = jnp.zeros((CH, 1), F32)
    for w in range(rows):
        sum_two += jnp.sum(cp_ref[w * CH : (w + 1) * CH].astype(F32), 1, keepdims=True)
    col = lax.broadcasted_iota(jnp.int32, (CH, 128), 1)
    all_ref[1728:1792] = jnp.where(col < 64, sum_one, sum_two * factor)
    if total > 1792:
        all_ref[1792:] = jnp.zeros((total - 1792, 128), F32)
    core = core_ref[0]
    side = total // 2
    keep_ref[...] = all_ref[pl.ds(pl.multiple_of(core * side, 8), side)]
    send_ref[...] = all_ref[pl.ds(pl.multiple_of((1 - core) * side, 8), side)].astype(BF)


def pair_kernel(keep_ref, got_ref, out_ref):
    out_ref[...] = (keep_ref[...] + got_ref[...].astype(F32)).astype(BF)


def reduce_kernel(parts, got_ref, out_ref):
    total = got_ref[0].astype(F32)
    for k in range(1, parts):
        total = total + got_ref[k].astype(F32)
    total = total.astype(BF)
    for k in range(parts):
        out_ref[k] = total


def unpack_kernel(total, core_ref, mine_ref, other_ref, g1_ref, b1_ref, g2_ref, b2_ref, all_ref):
    core = core_ref[0]
    side = total // 2
    all_ref[pl.ds(pl.multiple_of(core * side, 8), side)] = mine_ref[...].astype(F32)
    all_ref[pl.ds(pl.multiple_of((1 - core) * side, 8), side)] = other_ref[...].astype(F32)
    corner = all_ref[1344:1728]
    for w in range(3):
        for ns in range(9):
            t = (2 - w) * 9 + 8 - ns
            if w < 2:
                block = all_ref[ns * CH : (ns + 1) * CH, w * CH : (w + 1) * CH]
            elif ns < 6:
                block = corner[ns * CH : (ns + 1) * CH, :CH]
            else:
                block = corner[(ns - 6) * CH : (ns - 5) * CH, CH:]
            g2_ref[:, t * CH : (t + 1) * CH] = block
    for w in range(3):
        for k in range(4):
            block = all_ref[576 + 192 * k + w * CH : 576 + 192 * k + (w + 1) * CH]
            g1_ref[:, w * 576 + k * 128 : w * 576 + (k + 1) * 128] = block
        g1_ref[:, w * 576 + 512 : (w + 1) * 576] = corner[192 + w * CH : 192 + (w + 1) * CH, CH:]
    b1_ref[...] = all_ref[1728:1792, :1]
    b2_ref[...] = all_ref[1728:1792, 64:65]


def predict_kernel(rows, d_ref, hid_ref, up_ref, down_ref, w2_ref, b2_ref, out_ref, stack_ref, halo_ref, pad_ref, mid_ref, row_ref):
    rate = d_ref[1]
    local_part(rows, hid_ref, rate, w2_ref, stack_ref, mid_ref, pad_ref)
    pred = halo_part(rows, up_ref[...], down_ref[...], rate, w2_ref, halo_ref, mid_ref[...], pad_ref)
    pred = (pred + b2_ref[...]).astype(BF)
    for w in range(rows):
        row_ref[w * CH : (w + 1) * CH] = pred[:, w * NS : (w + 1) * NS]
    out_ref[...] = swap_rows(row_ref[...], rows, CH)


def by_row_tap(weight):
    return weight.reshape(CH, 3, 576).transpose(1, 0, 2).reshape(192, 576)


def body(inputs, cotangent, weight_one, bias_one, weight_two, bias_two, dilation):
    rows = inputs.shape[2]
    wrap = lax.axis_size("wrap")
    pairs = lax.axis_size("x")
    group = wrap * pairs
    factor = 1.0 / math.sqrt(inputs.shape[0] * pairs * 2 * rows * wrap * NS)
    piece = -(-1792 // (2 * group) // 8) * 8 if 1792 % (16 * group) else 1792 // (2 * group)
    piece = max(8, -(-(-(-1792 // (2 * group))) // 8) * 8)
    total = 2 * group * piece
    cells = rows * NS
    up = [(i, (i + 1) % wrap) for i in range(wrap)]
    down = [(j, i) for i, j in up]
    swap = [(0, 1), (1, 0)]
    core = lax.axis_index("core").astype(jnp.int32).reshape(1)
    half = DMAX * CH

    x2 = inputs.reshape(CH * rows, NS)
    c2 = cotangent.reshape(CH * rows, NS)
    flat = sds((rows * CH, NS), BF)
    xp, cp, top, bottom = call(
        lambda *refs: prep_kernel(rows, *refs),
        (flat, flat, sds((2 * half, NS), BF), sds((2 * half, NS), BF)),
        ins=[VM, VM],
        name="prep",
    )(x2, c2)
    from_up = lax.ppermute(bottom, "wrap", up)
    from_down = lax.ppermute(top, "wrap", down)

    w1 = by_row_tap(weight_one)
    w2 = by_row_tap(weight_two)
    flip = jnp.transpose(weight_two.reshape(CH, 27, CH)[:, ::-1, :], (2, 1, 0)).reshape(CH, 27 * CH)
    wf = by_row_tap(flip)

    stack = sds((576, cells), BF)
    part = sds((CH, cells), F32)
    ext = (rows + 2 * DMAX) * NS
    xs, cs, pre, back = call(
        lambda *refs: local_kernel(rows, *refs),
        (stack, stack, part, part),
        scratch=[pltpu.VMEM((CH, ext), F32)],
        ins=[SM] + [VM] * 4,
        flops=4 * 10**9,
        nbytes=8 * 10**6,
        name="local",
    )(dilation, xp, cp, w1, wf)

    side = total // 2
    hid, keep, send = call(
        lambda *refs: grad_kernel(rows, total, factor, *refs),
        (flat, sds((side, 128), F32), sds((side, 128), BF)),
        scratch=[
            pltpu.VMEM((CH, ext), F32),
            pltpu.VMEM((CH, (rows + 4 * DMAX) * NS), BF),
            pltpu.VMEM((192, ext), BF),
            pltpu.VMEM((576, 2 * DMAX * NS), BF),
            pltpu.VMEM((576, 2 * DMAX * NS), BF),
            pltpu.VMEM((total, 128), F32),
        ],
        ins=[SM, SM] + [VM] * 10,
        flops=4 * 10**9,
        nbytes=8 * 10**6,
        name="grads",
    )(dilation, core, bias_one.reshape(CH, 1), from_up, from_down, w1, wf, xs, cs, pre, back, cp)

    got = lax.ppermute(send, "core", swap)
    hid_up = lax.ppermute(hid[rows * CH - half :], "wrap", up)
    hid_down = lax.ppermute(hid[:half], "wrap", down)
    both = call(pair_kernel, sds((side, 128), BF), ins=[VM, VM], name="pair")(keep, got)
    parts = lax.all_to_all(both.reshape(group, piece, 128), ("wrap", "x"), 0, 0, tiled=True)
    mine = call(
        lambda *refs: reduce_kernel(group, *refs),
        sds((group, piece, 128), BF),
        ins=[VM],
        name="reduce",
    )(parts)
    gathered = lax.all_to_all(mine, ("wrap", "x"), 0, 0, tiled=True).reshape(side, 128)
    other = lax.ppermute(gathered, "core", swap)
    g1, b1, g2, b2 = call(
        lambda *refs: unpack_kernel(total, *refs),
        (sds((CH, 1728), F32), sds((CH, 1), F32), sds((CH, 1728), F32), sds((CH, 1), F32)),
        scratch=[pltpu.VMEM((total, 128), F32)],
        ins=[SM, VM, VM],
        name="unpack",
    )(core, gathered, other)

    pred = call(
        lambda *refs: predict_kernel(rows, *refs),
        flat,
        scratch=[
            pltpu.VMEM((576, cells), BF),
            pltpu.VMEM((576, 2 * DMAX * NS), BF),
            pltpu.VMEM((CH, ext), F32),
            pltpu.VMEM((CH, cells), F32),
            pltpu.VMEM((rows * CH, NS), BF),
        ],
        ins=[SM] + [VM] * 5,
        flops=4 * 10**9,
        nbytes=10**6,
        name="predict",
    )(dilation, hid, hid_up, hid_down, w2, bias_two.reshape(CH, 1))
    return (
        pred.reshape(1, CH, rows, NS),
        g1,
        b1.reshape(CH),
        g2,
        b2.reshape(CH),
    )


def solution(mesh):
    wrap, samp = mesh.devices.shape
    split = Mesh(mesh.devices.reshape(wrap, samp // 2, 2), ("wrap", "x", "core"))
    field = P(("x", "core"), None, "wrap", None)
    return jax.shard_map(
        body,
        mesh=split,
        in_specs=(field, field, P(), P(), P(), P(), P()),
        out_specs=(field, P(), P(), P(), P()),
        check_vma=False,
    )
```

time: 351 us -> 77.7 us (0.22)
  waiting for transfers between devices: 127 us -> 6.76 us
  local copies, waits for them, and re-layouts: 108 us -> 9.05 us
  matrix products: 28.9 us -> 0 us
  Pallas kernels: 0 us -> 27.9 us
  blocking collectives: 40.3 us -> 15.4 us
  between operations: 19.6 us -> 0.75 us
  other arithmetic: 7.83 us -> 2.77 us
    psum x1 -> x0, waiting for transfers between devices: 126 us -> none  [body(): lax.psum((grad_one, bias_one_grad, grad_two, bias_two_grad), ('wrap', 'sa...]
    concatenate x11 -> x0, local copies, waits for them, and re-layouts: 50.9 us -> none  [the longest x9 47 us: tap_stack(): return jnp.concatenate(windows, 0)]
    psum x1 -> x0, blocking collectives: 40.3 us -> none  [body(): lax.psum((grad_one, bias_one_grad, grad_two, bias_two_grad), ('wrap', 'sa...]
    dot_general x15 -> x0, matrix products: 28.9 us -> none  [the longest x9 22 us: convolve(): jnp.dot(weight[:, tap_w * 9 * in_chan:(tap_w + 1) * 9 * in_chan], stacked...]
    pallas_call x0 -> x7, Pallas kernels: none -> 27.9 us  [the longest x1 9.43 us: body(): call(lambda *refs: grad_kernel(rows, total, factor, *refs), (flat, sds((s...]
    dynamic_slice x5 -> x0, local copies, waits for them, and re-layouts: 25.5 us -> none  [tap_stack(): window = lax.dynamic_slice(padded, offsets, (in_chan, out_rows, NR, S))]
    all_to_all x0 -> x1, blocking collectives: none -> 15.4 us  [body(): lax.all_to_all(both.reshape(group, piece, 128), ('wrap', 'x'), 0, 0, tile...]
    reshape x10 -> x5, local copies, waits for them, and re-layouts: 15.4 us -> 3.16 us  [the longest x1 1.41 us: body(): weight_two.reshape(CH, 27, CH)[:, ::-1, :]]
  transfers between devices with their start and end apart: 7 -> 7, of which waited for: 2 -> 4; matrix products, arithmetic and copies ran while one was open for 6% -> 8% of each run, Pallas kernels for 0% -> 13%
where the time goes in v1:
time: 77.7 us; the launch traced here: 77.1 us
  Pallas kernels  27.9 us (36%)
  blocking collectives  15.4 us (20%)
  starting transfers between devices  14.6 us (19%)
  local copies, waits for them, and re-layouts  9.05 us (12%)
  waiting for transfers between devices  6.76 us (9%)
  other arithmetic  2.77 us (4%)
    all_to_all x1, blocking collectives, body(): lax.all_to_all(both.reshape(group, piece, 128), ('wrap', 'x'), 0, 0, tile...  15.4 us
    pallas_call x1, Pallas kernels, body(): call(lambda *refs: grad_kernel(rows, total, factor, *refs), (flat, sds((s...  9.43 us
    pallas_call x1, Pallas kernels, body(): call(lambda *refs: local_kernel(rows, *refs), (stack, stack, part, part),...  5.28 us
    pallas_call x1, Pallas kernels, body(): call(lambda *refs: predict_kernel(rows, *refs), flat, scratch=[pltpu.VMEM...  5 us
    all_to_all x1, waiting for transfers between devices, body(): lax.all_to_all(mine, ('wrap', 'x'), 0, 0, tiled=True).reshape(side, 128)  3.71 us
    all_to_all x1, starting transfers between devices, body(): lax.all_to_all(mine, ('wrap', 'x'), 0, 0, tiled=True).reshape(side, 128)  3.53 us
    ppermute x1, starting transfers between devices, body(): from_down = lax.ppermute(top, 'wrap', down)  3.07 us
    ppermute x1, starting transfers between devices, body(): from_up = lax.ppermute(bottom, 'wrap', up)  3 us
  transfers between devices with their start and end apart: 7, of which 4 were waited for; matrix products, arithmetic and copies ran while one was open for 8% of the time, Pallas kernels for 13%

profile of v1, /device:TPU:0, one launch (start us, length us, event | category | flops | bytes accessed | tf_op | source)
XLA Modules:
  0.0 77.1 jit_solution(14886675797301097284)
XLA Ops:
  0.6 0.0 copy-start.4
  0.6 2.5 %prep.1 = (bf16[512,256]{1,0:T(8,128)(2,1)}, bf16[512,256]{1,0:T(8,128)(2,1)}, bf16[512,256]{1,0:T(8,128)(2,1)}, bf16[512,256]{1,0:T(8,128)(2,1)}) custom-call(bf16[512,256]{1,0:T(8,128)(2,1)} %bitcast.24, bf16[512,256]{1,0:T(8,128)(2,1)} %bitcast.25), custom_call_target="tpu_custom_call" | custom-call | tf_op jit(solution)/shard_map/prep/pallas_call | solution.py:249
  3.1 0.0 copy-start.6
  3.1 3.0 %collective-permute-start = (bf16[512,256]{1,0:T(8,128)(2,1)}, bf16[512,256]{1,0:T(8,128)(2,1)S(1)}, u32[]{:S(2)}, u32[]{:S(2)}) collective-permute-start(bf16[512,256]{1,0:T(8,128)(2,1)} %get-tuple-element.20), channel_id=1, source_target_pairs={{0,4},{4,8},{8,12},{12,16},{16,20},{20,24},{24,28},{28,0},{1,5},{5... | collective-permute-start | bytes 786440 | tf_op jit(solution)/shard_map/ppermute | solution.py:255
  6.1 3.1 %collective-permute-start.1 = (bf16[512,256]{1,0:T(8,128)(2,1)}, bf16[512,256]{1,0:T(8,128)(2,1)S(1)}, u32[]{:S(2)}, u32[]{:S(2)}) collective-permute-start(bf16[512,256]{1,0:T(8,128)(2,1)} %get-tuple-element.21), channel_id=1, source_target_pairs={{4,0},{8,4},{12,8},{16,12},{20,16},{24,20},{28,24},{0,28},{5,1},{9... | collective-permute-start | bytes 786440 | tf_op jit(solution)/shard_map/ppermute | solution.py:256
  9.2 1.4 %reshape.64 = bf16[64,27,64]{2,1,0:T(8,128)(2,1)S(1)} reshape(bf16[64,1728]{1,0:T(8,128)(2,1)} %param.11) | data formatting | bytes 442368 | tf_op jit(solution)/shard_map/reshape | solution.py:260
  10.6 0.5 rev.3
  11.1 0.2 copy.17
  11.3 0.9 %copy.18 = bf16[3,64,576]{2,1,0:T(8,128)(2,1)} copy(bf16[3,64,576]{1,2,0:T(8,128)(2,1)S(1)} %bitcast.18) | data formatting | bytes 442368 | tf_op jit(solution)/shard_map/transpose | solution.py:227
  12.2 0.0 copy-done.4
  12.2 0.2 reshape.62
  12.4 0.7 copy.16
  13.2 0.0 copy-done.6
  13.2 0.7 copy.19.refs_2_
  13.9 5.3 %local.1 = (bf16[576,2048]{1,0:T(8,128)(2,1)}, bf16[576,2048]{1,0:T(8,128)(2,1)}, f32[64,2048]{1,0:T(8,128)}, f32[64,2048]{1,0:T(8,128)}) custom-call(s32[2]{0:T(128)} %refs_0_.5, bf16[512,256]{1,0:T(8,128)(2,1)} %get-tuple-element.22.refs_1_, bf16[512,256]{1,0:T(8,128)(2,1)} %get-tuple-element.23.refs_2_.refs_11_, bf16[192,576]{1,0:T(8,128)(2,1)} %bitcast.26, ...), custom_call_target="tpu_custom_call" | custom-call | flops 4000000000 | bytes 8000000 | tf_op jit(solution)/shard_map/local/pallas_call | solution.py:266
  19.1 0.0 collective-permute-done.refs_3_
  19.1 0.0 copy-start.8
  19.1 0.6 collective-permute-done.1.refs_4_
  19.7 0.0 copy-start.9
  19.7 0.1 copy-done.8
  19.8 0.6 copy-done.9
  20.4 9.4 %grads.1 = (bf16[512,256]{1,0:T(8,128)(2,1)}, f32[896,128]{1,0:T(8,128)}, bf16[896,128]{1,0:T(8,128)(2,1)}) custom-call(s32[2]{0:T(128)} %refs_0_.5, s32[1]{0:T(128)} %bitcast.refs_1_.refs_0_, f32[64,1]{1,0:T(8,128)} %copy.19.refs_2_, bf16[512,256]{1,0:T(8,128)(2,1)} %copy-done.8, bf16[512,256]{1,0:T(8,128)(2,1)} %copy-done.9, bf16[192,576]{1,0:T(8,128)(2,1)} %bitcast.27, ...), custom_call_target="tpu_custom_call" | custom-call | flops 4000000000 | bytes 8000000 | tf_op jit(solution)/shard_map/grads/pallas_call | solution.py:277
  29.8 0.0 copy-start.2
  29.8 0.0 copy-start.1
  29.9 0.0 copy-start.7
  29.9 0.1 collective-permute-start.4
  29.9 1.7 %collective-permute-done.4.got_ref = bf16[896,128]{1,0:T(8,128)(2,1)S(1)} collective-permute-done((bf16[896,128]{1,0:T(8,128)(2,1)}, bf16[896,128]{1,0:T(8,128)(2,1)S(1)}, u32[]{:S(2)}, u32[]{:S(2)}) %collective-permute-start.4) | collective-permute-done | bytes 229408 | tf_op jit(solution)/shard_map/ppermute | solution.py:294
  31.6 0.0 copy-start.3
  31.6 0.7 copy-done.3
  32.3 1.8 %pair.1 = bf16[896,128]{1,0:T(8,128)(2,1)} custom-call(f32[896,128]{1,0:T(8,128)} %get-tuple-element.29.keep_ref, bf16[896,128]{1,0:T(8,128)(2,1)} %copy-done.3), custom_call_target="tpu_custom_call" | custom-call | tf_op jit(solution)/shard_map/pair/pallas_call | solution.py:297
  34.1 15.4 %all_to_all.10.refs_0_ = bf16[16,56,128]{2,1,0:T(8,128)(2,1)} all-to-all(bf16[16,56,128]{2,1,0:T(8,128)(2,1)} %bitcast.21), channel_id=1, replica_groups=mesh['wrap'=8,'x'=2,'core'=2] {'wrap','x'}, dimensions={0} | all-to-all | bytes 458752 | tf_op jit(solution)/shard_map/all_to_all | solution.py:298
  49.5 1.7 %reduce.3 = bf16[16,56,128]{2,1,0:T(8,128)(2,1)} custom-call(bf16[16,56,128]{2,1,0:T(8,128)(2,1)} %all_to_all.10.refs_0_), custom_call_target="tpu_custom_call" | custom-call | tf_op jit(solution)/shard_map/reduce/pallas_call | solution.py:299
  51.2 3.5 %all-to-all-start.1 = ((bf16[16,56,128]{2,1,0:T(8,128)(2,1)}), bf16[16,56,128]{2,1,0:T(8,128)(2,1)S(1)}, u32[]{:S(2)}, u32[]{:S(2)}) async-start(bf16[16,56,128]{2,1,0:T(8,128)(2,1)} %reduce.3), calls=%async_computation.1 | async-start | bytes 458752 | tf_op jit(solution)/shard_map/all_to_all | solution.py:305
  54.7 0.0 copy-done.2
  54.7 1.9 %collective-permute-start.2 = (bf16[256,256]{1,0:T(8,128)(2,1)S(1)}, bf16[256,256]{1,0:T(8,128)(2,1)S(1)}, u32[]{:S(2)}, u32[]{:S(2)}) collective-permute-start(bf16[256,256]{1,0:T(8,128)(2,1)S(1)} %get-tuple-element.36), channel_id=1, source_target_pairs={{0,4},{4,8},{8,12},{12,16},{16,20},{20,24},{24,28},{28,0},{1,5},{5... | collective-permute-start | bytes 393224 | tf_op jit(solution)/shard_map/ppermute | solution.py:295
  56.6 3.0 %collective-permute-start.3 = (bf16[256,256]{1,0:T(8,128)(2,1)S(1)}, bf16[256,256]{1,0:T(8,128)(2,1)S(1)}, u32[]{:S(2)}, u32[]{:S(2)}) collective-permute-start(bf16[256,256]{1,0:T(8,128)(2,1)S(1)} %get-tuple-element.35), channel_id=1, source_target_pairs={{4,0},{8,4},{12,8},{16,12},{20,16},{24,20},{28,24},{0,28},{5,1},{9... | collective-permute-start | bytes 393224 | tf_op jit(solution)/shard_map/ppermute | solution.py:296
  59.6 0.0 copy-done.1
  59.6 0.2 reshape.66
  59.8 0.7 copy.20
  60.5 0.0 copy-done.7
  60.5 0.7 copy.21.refs_5_
  61.2 3.7 %all-to-all-done.1 = bf16[16,56,128]{2,1,0:T(8,128)(2,1)S(1)} async-done(((bf16[16,56,128]{2,1,0:T(8,128)(2,1)}), bf16[16,56,128]{2,1,0:T(8,128)(2,1)S(1)}, u32[]{:S(2)}, u32[]{:S(2)}) %all-to-all-start.1) | async-done | bytes 229408 | tf_op jit(solution)/shard_map/all_to_all | solution.py:305
  65.0 0.0 copy-start
  65.0 0.0 collective-permute-start.5
  65.0 0.8 %collective-permute-done.2.refs_2_ = bf16[256,256]{1,0:T(8,128)(2,1)S(1)} collective-permute-done((bf16[256,256]{1,0:T(8,128)(2,1)S(1)}, bf16[256,256]{1,0:T(8,128)(2,1)S(1)}, u32[]{:S(2)}, u32[]{:S(2)}) %collective-permute-start.2) | collective-permute-done | bytes 131104 | tf_op jit(solution)/shard_map/ppermute | solution.py:295
  65.7 0.0 copy-start.10
  65.7 0.0 collective-permute-done.3.refs_3_
  65.8 0.0 copy-start.11
  65.8 0.6 copy-done.10
  66.4 0.0 copy-done.11
  66.4 5.0 %predict.1 = bf16[512,256]{1,0:T(8,128)(2,1)} custom-call(s32[2]{0:T(128)} %refs_0_.5, bf16[512,256]{1,0:T(8,128)(2,1)} %get-tuple-element.28.refs_1_, bf16[256,256]{1,0:T(8,128)(2,1)} %copy-done.10, bf16[256,256]{1,0:T(8,128)(2,1)} %copy-done.11, bf16[192,576]{1,0:T(8,128)(2,1)} %bitcast.28, f32[64,1]{1,0:T(8,128)} %copy.21.refs_5_), custom_call_target="tpu_custom_call" | custom-call | flops 4000000000 | bytes 1000000 | tf_op jit(solution)/shard_map/predict/pallas_call | solution.py:315
  71.4 0.0 copy-done
  71.4 0.0 collective-permute-done.5.refs_2_
  71.4 0.0 copy-start.5
  71.4 0.7 copy-done.5
  72.1 2.2 %unpack.1 = (f32[64,1728]{1,0:T(8,128)}, f32[64,1]{1,0:T(8,128)}, f32[64,1728]{1,0:T(8,128)}, f32[64,1]{1,0:T(8,128)}) custom-call(s32[1]{0:T(128)} %bitcast.refs_1_.refs_0_, bf16[896,128]{1,0:T(8,128)(2,1)} %bitcast.23, bf16[896,128]{1,0:T(8,128)(2,1)} %copy-done.5), custom_call_target="tpu_custom_call" | custom-call | tf_op jit(solution)/shard_map/unpack/pallas_call | solution.py:307
  74.3 1.4 %reduce.1 = f32[64]{0:T(128)} reduce(f32[64,1]{1,0:T(8,128)} %get-tuple-element.32, f32[]{:T(128)} %constant.6), dimensions={1}, to_apply=%get-tuple-element.32.reduce_sub_computation | reduce | bytes 516 | tf_op jit(solution)/shard_map/unpack/pallas_call | solution.py:307
  75.7 1.4 %reduce.2 = f32[64]{0:T(128)} reduce(f32[64,1]{1,0:T(8,128)} %get-tuple-element.34, f32[]{:T(128)} %constant.6), dimensions={1}, to_apply=%get-tuple-element.34.reduce_sub_computation | reduce | bytes 516 | tf_op jit(solution)/shard_map/unpack/pallas_call | solution.py:307
  (1 shorter events, 0.0 us)
Async XLA Ops:
  0.6 11.6 %copy-start.4 = (bf16[64,1728]{1,0:T(8,128)(2,1)S(1)}, bf16[64,1728]{1,0:T(8,128)(2,1)}, u32[]{:S(2)}) copy-start(bf16[64,1728]{1,0:T(8,128)(2,1)} %param.9) | copy-start | bytes 663556
  3.1 10.0 %copy-start.6 = (f32[64]{0:T(128)S(1)}, f32[64]{0:T(128)}, u32[]{:S(2)}) copy-start(f32[64]{0:T(128)} %param.10) | copy-start | bytes 772
  3.1 16.0 %collective-permute-start = (bf16[512,256]{1,0:T(8,128)(2,1)}, bf16[512,256]{1,0:T(8,128)(2,1)S(1)}, u32[]{:S(2)}, u32[]{:S(2)}) collective-permute-start(bf16[512,256]{1,0:T(8,128)(2,1)} %get-tuple-element.20), channel_id=1, source_target_pairs={{0,4},{4,8},{8,12},{12,16},{16,20},{20,24},{24,28},{28,0},{1,5},{5... | collective-permute-start | bytes 786440 | tf_op jit(solution)/shard_map/ppermute | solution.py:255
  6.1 13.6 %collective-permute-start.1 = (bf16[512,256]{1,0:T(8,128)(2,1)}, bf16[512,256]{1,0:T(8,128)(2,1)S(1)}, u32[]{:S(2)}, u32[]{:S(2)}) collective-permute-start(bf16[512,256]{1,0:T(8,128)(2,1)} %get-tuple-element.21), channel_id=1, source_target_pairs={{4,0},{8,4},{12,8},{16,12},{20,16},{24,20},{28,24},{0,28},{5,1},{9... | collective-permute-start | bytes 786440 | tf_op jit(solution)/shard_map/ppermute | solution.py:256
  19.1 0.7 copy-start.8
  19.7 0.7 copy-start.9
  29.8 24.9 %copy-start.2 = (bf16[512,256]{1,0:T(8,128)(2,1)S(1)}, bf16[512,256]{1,0:T(8,128)(2,1)}, u32[]{:S(2)}) copy-start(bf16[512,256]{1,0:T(8,128)(2,1)} %get-tuple-element.28.refs_1_) | copy-start | bytes 786436
  29.8 29.8 %copy-start.1 = (bf16[64,1728]{1,0:T(8,128)(2,1)S(1)}, bf16[64,1728]{1,0:T(8,128)(2,1)}, u32[]{:S(2)}) copy-start(bf16[64,1728]{1,0:T(8,128)(2,1)} %param.11) | copy-start | bytes 663556
  29.9 30.7 %copy-start.7 = (f32[64]{0:T(128)S(1)}, f32[64]{0:T(128)}, u32[]{:S(2)}) copy-start(f32[64]{0:T(128)} %param.12) | copy-start | bytes 772
  29.9 1.8 %collective-permute-start.4 = (bf16[896,128]{1,0:T(8,128)(2,1)}, bf16[896,128]{1,0:T(8,128)(2,1)S(1)}, u32[]{:S(2)}, u32[]{:S(2)}) collective-permute-start(bf16[896,128]{1,0:T(8,128)(2,1)} %get-tuple-element.30), channel_id=1, source_target_pairs={{0,1},{1,0},{2,3},{3,2},{4,5},{5,4},{6,7},{7,6},{8,9},{9,8},{10,11... | collective-permute-start | bytes 688136 | tf_op jit(solution)/shard_map/ppermute | solution.py:294
  31.6 0.7 copy-start.3
  51.2 13.8 %all-to-all-start.1 = ((bf16[16,56,128]{2,1,0:T(8,128)(2,1)}), bf16[16,56,128]{2,1,0:T(8,128)(2,1)S(1)}, u32[]{:S(2)}, u32[]{:S(2)}) async-start(bf16[16,56,128]{2,1,0:T(8,128)(2,1)} %reduce.3), calls=%async_computation.1 | async-start | bytes 458752 | tf_op jit(solution)/shard_map/all_to_all | solution.py:305
  54.7 11.0 %collective-permute-start.2 = (bf16[256,256]{1,0:T(8,128)(2,1)S(1)}, bf16[256,256]{1,0:T(8,128)(2,1)S(1)}, u32[]{:S(2)}, u32[]{:S(2)}) collective-permute-start(bf16[256,256]{1,0:T(8,128)(2,1)S(1)} %get-tuple-element.36), channel_id=1, source_target_pairs={{0,4},{4,8},{8,12},{12,16},{16,20},{20,24},{24,28},{28,0},{1,5},{5... | collective-permute-start | bytes 393224 | tf_op jit(solution)/shard_map/ppermute | solution.py:295
  56.6 9.1 %collective-permute-start.3 = (bf16[256,256]{1,0:T(8,128)(2,1)S(1)}, bf16[256,256]{1,0:T(8,128)(2,1)S(1)}, u32[]{:S(2)}, u32[]{:S(2)}) collective-permute-start(bf16[256,256]{1,0:T(8,128)(2,1)S(1)} %get-tuple-element.35), channel_id=1, source_target_pairs={{4,0},{8,4},{12,8},{16,12},{20,16},{24,20},{28,24},{0,28},{5,1},{9... | collective-permute-start | bytes 393224 | tf_op jit(solution)/shard_map/ppermute | solution.py:296
  65.0 6.5 %copy-start = (bf16[16,56,128]{2,1,0:T(8,128)(2,1)}, bf16[16,56,128]{2,1,0:T(8,128)(2,1)S(1)}, u32[]{:S(2)}) copy-start(bf16[16,56,128]{2,1,0:T(8,128)(2,1)S(1)} %all-to-all-done.1) | copy-start | bytes 688132
  65.0 6.5 %collective-permute-start.5 = (bf16[896,128]{1,0:T(8,128)(2,1)S(1)}, bf16[896,128]{1,0:T(8,128)(2,1)S(1)}, u32[]{:S(2)}, u32[]{:S(2)}) collective-permute-start(bf16[896,128]{1,0:T(8,128)(2,1)S(1)} %bitcast.22), channel_id=1, source_target_pairs={{0,1},{1,0},{2,3},{3,2},{4,5},{5,4},{6,7},{7,6},{8,9},{9,8},{10,11... | collective-permute-start | bytes 688136 | tf_op jit(solution)/shard_map/ppermute | solution.py:306
  65.7 0.7 copy-start.10
  65.8 0.7 copy-start.11
  71.4 0.7 copy-start.5

commit v2 on v1

v2 whole, which is shorter than its diff:
```python
import math

import jax
import jax.numpy as jnp
from jax import lax
from jax.experimental import pallas as pl
from jax.experimental.pallas import tpu as pltpu
from jax.sharding import Mesh
from jax.sharding import PartitionSpec as P

DMAX = 4
NR = 16
S = 16
NS = NR * S
CH = 64
TAPS = 9 * CH
HALF = DMAX * CH
NEAR = DMAX * NS
BF = jnp.bfloat16
F32 = jnp.float32

VM = pl.BlockSpec(memory_space=pltpu.VMEM)
SM = pl.BlockSpec(memory_space=pltpu.SMEM)
ANY = pl.BlockSpec(memory_space=pl.ANY)


def sds(shape, dtype):
    return jax.ShapeDtypeStruct(shape, dtype)


def call(kernel, outs, scratch=(), ins=None, flops=10**8, nbytes=10**6, name=None, mib=24):
    return pl.pallas_call(
        kernel,
        out_shape=outs,
        in_specs=ins,
        out_specs=jax.tree.map(lambda _: VM, outs),
        scratch_shapes=list(scratch),
        cost_estimate=pl.CostEstimate(flops=flops, bytes_accessed=nbytes, transcendentals=0),
        compiler_params=pltpu.CompilerParams(vmem_limit_bytes=mib * 1024 * 1024),
        name=name,
    )


def nt(a, b):
    return lax.dot_general(a, b, (((1,), (1,)), ((), ())), preferred_element_type=F32)


def mm(a, b):
    return jnp.dot(a, b, preferred_element_type=F32)


def select_matrix(rows, cols, target):
    src = lax.broadcasted_iota(jnp.int32, (rows, cols), 0)
    return jnp.where(src == target, 1.0, 0.0).astype(BF)


def shift_matrices(rate, out_ref):
    dst = lax.broadcasted_iota(jnp.int32, (1, NS), 1)
    for tap in range(9):
        dn = tap // 3 - 1
        ds = tap % 3 - 1
        span = (dst & (S - 1)) + ds * rate
        target = jnp.where((span >= 0) & (span < S), dst + (dn * S + ds) * rate, -1)
        out_ref[tap * NS : (tap + 1) * NS] = select_matrix(NS, NS, target)


def row_swap_matrix(major, minor):
    size = major * minor
    dst = lax.broadcasted_iota(jnp.int32, (size, 1), 0)
    want = (dst % major) * minor + dst // major
    src = lax.broadcasted_iota(jnp.int32, (size, size), 1)
    return jnp.where(src == want, 1.0, 0.0).astype(BF)


def shifted(x, mats_ref, stack_ref):
    rows = x.shape[0] // CH
    for tap in range(9):
        moved = x if tap == 4 else mm(x, mats_ref[tap * NS : (tap + 1) * NS]).astype(BF)
        for w in range(rows):
            stack_ref[tap * CH : (tap + 1) * CH, w * NS : (w + 1) * NS] = moved[w * CH : (w + 1) * CH]


def lanes(row, count):
    return pl.ds(pl.multiple_of(row * NS, NS), count * NS)


def column(row):
    i = lax.broadcasted_iota(jnp.int32, (CH, CH), 0)
    j = lax.broadcasted_iota(jnp.int32, (CH, CH), 1)
    return jnp.sum(jnp.where(i == j, jnp.broadcast_to(row, (CH, CH)), 0.0), 1, keepdims=True)


def prep_kernel(rows, par_ref, x_ref, c_ref, xp_ref, cp_ref, a_ref, b_ref):
    even = par_ref[0] == 0
    last = rows * CH - HALF
    first_at = pl.ds(pl.multiple_of(jnp.where(even, last, 0), CH), HALF)
    second_at = pl.ds(pl.multiple_of(jnp.where(even, 0, last), CH), HALF)
    perm = row_swap_matrix(CH, rows)
    for k, (src, dst) in enumerate(((x_ref, xp_ref), (c_ref, cp_ref))):
        dst[...] = mm(perm, src[...]).astype(BF)
        a_ref[k * HALF : (k + 1) * HALF] = dst[first_at]
        b_ref[k * HALF : (k + 1) * HALF] = dst[second_at]


def rows_by_tap(w_ref, out_ref):
    for w in range(3):
        out_ref[w * CH : (w + 1) * CH] = w_ref[:, w * TAPS : (w + 1) * TAPS]


def flipped_rows(w_ref, out_ref):
    turned = w_ref[...].astype(F32).T.astype(BF)
    for w in range(3):
        blocks = []
        for ns in range(9):
            t = (2 - w) * 9 + 8 - ns
            blocks.append(turned[t * CH : (t + 1) * CH])
        out_ref[w * CH : (w + 1) * CH] = jnp.concatenate(blocks, 1)


def local_part(rows, x, rate, w_ref, mats_ref, stack_ref, part_ref, pad_ref):
    shifted(x, mats_ref, stack_ref)
    pad_ref[:, :NEAR] = jnp.zeros((CH, NEAR), F32)
    pad_ref[:, NEAR + rows * NS :] = jnp.zeros((CH, NEAR), F32)
    z = mm(w_ref[...], stack_ref[...])
    pad_ref[:, NEAR : NEAR + rows * NS] = z[CH : 2 * CH]
    pad_ref[:, lanes(DMAX + rate, rows)] += z[:CH]
    pad_ref[:, lanes(DMAX - rate, rows)] += z[2 * CH :]
    part_ref[...] = pad_ref[:, NEAR : NEAR + rows * NS]


def local_kernel(
    rows,
    d_ref, xp_ref, cp_ref, one_ref, two_ref,
    xs_ref, cs_ref, pre_ref, back_ref, w1_ref, wf_ref, m1_ref, m2_ref,
    pad_ref,
):
    shift_matrices(d_ref[0], m1_ref)
    shift_matrices(d_ref[1], m2_ref)
    rows_by_tap(one_ref, w1_ref)
    flipped_rows(two_ref, wf_ref)
    local_part(rows, xp_ref[...], d_ref[0], w1_ref, m1_ref, xs_ref, pre_ref, pad_ref)
    local_part(rows, cp_ref[...], d_ref[1], wf_ref, m2_ref, cs_ref, back_ref, pad_ref)


def halo_part(rows, before, after, rate, w_ref, mats_ref, stack_ref, part, pad_ref):
    shifted(jnp.concatenate([before, after], 0), mats_ref, stack_ref)
    pad_ref[:, NEAR : NEAR + rows * NS] = part
    pad_ref[:, lanes(rate, DMAX)] += mm(w_ref[:CH], stack_ref[:, :NEAR])
    pad_ref[:, lanes(DMAX + rows - rate, DMAX)] += mm(w_ref[2 * CH :], stack_ref[:, NEAR:])
    return pad_ref[:, NEAR : NEAR + rows * NS]


def triple(rows, value, rate, pad_ref, out_ref):
    cells = rows * NS
    pad_ref[:, : 2 * NEAR] = jnp.zeros((CH, 2 * NEAR), BF)
    pad_ref[:, 2 * NEAR + cells :] = jnp.zeros((CH, 2 * NEAR), BF)
    pad_ref[:, 2 * NEAR : 2 * NEAR + cells] = value
    out_ref[:CH] = pad_ref[:, lanes(2 * DMAX + rate, rows)]
    out_ref[CH : 2 * CH] = value
    out_ref[2 * CH :] = pad_ref[:, lanes(2 * DMAX - rate, rows)]
    return pad_ref[:, lanes(DMAX + rate, DMAX)], pad_ref[:, lanes(2 * DMAX + rows - rate, DMAX)]


def grad_kernel(
    rows, total, factor,
    d_ref, core_ref, par_ref, b1_ref, a_ref, b_ref, w1_ref, wf_ref, xs_ref, cs_ref, pre_ref, back_ref, m1_ref, m2_ref,
    hid_ref, ha_ref, hb_ref, keep_ref, send_ref,
    pad_ref, pad16_ref, tri_ref, xh_ref, ch_ref, all_ref,
):
    r1 = d_ref[0]
    r2 = d_ref[1]
    even = par_ref[0] == 0
    cells = rows * NS
    one = a_ref[...]
    two = b_ref[...]
    up = jnp.where(even, two, one)
    down = jnp.where(even, one, two)
    pre = halo_part(rows, up[:HALF], down[:HALF], r1, w1_ref, m1_ref, xh_ref, pre_ref[...], pad_ref)
    pre = pre + column(b1_ref[...])
    sigm = 1.0 / (1.0 + jnp.exp(-pre))
    hidden = (pre * sigm).astype(BF)
    for w in range(rows):
        hid_ref[w * CH : (w + 1) * CH] = hidden[:, w * NS : (w + 1) * NS]
    last = rows * CH - HALF
    ha_ref[...] = hid_ref[pl.ds(pl.multiple_of(jnp.where(even, last, 0), CH), HALF)]
    hb_ref[...] = hid_ref[pl.ds(pl.multiple_of(jnp.where(even, 0, last), CH), HALF)]
    slope = sigm * (1.0 + pre * (1.0 - sigm))
    back = halo_part(rows, up[HALF:], down[HALF:], r2, wf_ref, m2_ref, ch_ref, back_ref[...], pad_ref)
    back_pre = (back * slope).astype(BF)

    before, after = triple(rows, hidden, r2, pad16_ref, tri_ref)
    g2 = nt(cs_ref[...], tri_ref[...])
    g2a = nt(ch_ref[:, :NEAR], before)
    g2b = nt(ch_ref[:, NEAR:], after)
    all_ref[:TAPS] = jnp.concatenate([g2[:, :CH] + g2a, g2[:, CH : 2 * CH]], 1) * factor
    left2 = (g2[:, 2 * CH :] + g2b) * factor

    before, after = triple(rows, back_pre, r1, pad16_ref, tri_ref)
    g1 = nt(tri_ref[...], xs_ref[...])
    g1a = nt(before, xh_ref[:, :NEAR])
    g1b = nt(after, xh_ref[:, NEAR:])
    g1 = jnp.concatenate([g1[:CH] + g1a, g1[CH : 2 * CH], g1[2 * CH :] + g1b], 0) * factor
    for k in range(4):
        all_ref[576 + 192 * k : 768 + 192 * k] = g1[:, 128 * k : 128 * (k + 1)]
    right = jnp.concatenate([left2[384:], g1[:, 512:]], 0)
    all_ref[1344:1728] = jnp.concatenate([left2[:384], right], 1)
    ones = jnp.ones((8, cells), BF)
    sums = jnp.concatenate([nt(ones, back_pre), nt(ones, cs_ref[4 * CH : 5 * CH])], 1)
    all_ref[1728:1736] = sums * factor
    all_ref[1736:] = jnp.zeros((total - 1736, 128), F32)
    core = core_ref[0]
    side = total // 2
    keep_ref[...] = all_ref[pl.ds(pl.multiple_of(core * side, 8), side)]
    send_ref[...] = all_ref[pl.ds(pl.multiple_of((1 - core) * side, 8), side)].astype(BF)


def pair_kernel(keep_ref, got_ref, out_ref):
    out_ref[...] = (keep_ref[...] + got_ref[...].astype(F32)).astype(BF)


def reduce_kernel(parts, got_ref, order_ref, out_ref):
    total = got_ref[0].astype(F32)
    for k in range(1, parts):
        total = total + got_ref[k].astype(F32)
    total = total.astype(BF)
    for k in range(parts):
        out_ref[k] = total


def unpack_kernel(total, core_ref, mine_ref, other_ref, g1_ref, b1_ref, g2_ref, b2_ref, all_ref):
    core = core_ref[0]
    side = total // 2
    all_ref[pl.ds(pl.multiple_of(core * side, 8), side)] = mine_ref[...].astype(F32)
    all_ref[pl.ds(pl.multiple_of((1 - core) * side, 8), side)] = other_ref[...].astype(F32)
    corner = all_ref[1344:1728]
    blocks = [None] * 27
    for w in range(3):
        for ns in range(9):
            if w < 2:
                block = all_ref[ns * CH : (ns + 1) * CH, w * CH : (w + 1) * CH]
            elif ns < 6:
                block = corner[ns * CH : (ns + 1) * CH, :CH]
            else:
                block = corner[(ns - 6) * CH : (ns - 5) * CH, CH:]
            blocks[(2 - w) * 9 + 8 - ns] = block
    g2_ref[...] = jnp.concatenate(blocks, 1)
    blocks = []
    for w in range(3):
        for k in range(4):
            blocks.append(all_ref[576 + 192 * k + w * CH : 576 + 192 * k + (w + 1) * CH])
        blocks.append(corner[192 + w * CH : 192 + (w + 1) * CH, CH:])
    g1_ref[...] = jnp.concatenate(blocks, 1)
    b1_ref[...] = all_ref[1728:1729, :CH]
    b2_ref[...] = all_ref[1728:1729, CH:]


def guess_kernel(rows, d_ref, hid_ref, two_ref, m2_ref, order_ref, part_ref, w2_ref, stack_ref, pad_ref):
    rows_by_tap(two_ref, w2_ref)
    local_part(rows, hid_ref[...], d_ref[1], w2_ref, m2_ref, stack_ref, part_ref, pad_ref)


def predict_kernel(
    rows, d_ref, par_ref, a_ref, b_ref, w2_ref, b2_ref, m2_ref, part_ref, out_ref, halo_ref, pad_ref, row_ref
):
    even = par_ref[0] == 0
    one = a_ref[...]
    two = b_ref[...]
    up = jnp.where(even, two, one)
    down = jnp.where(even, one, two)
    pred = halo_part(rows, up, down, d_ref[1], w2_ref, m2_ref, halo_ref, part_ref[...], pad_ref)
    pred = (pred + column(b2_ref[...])).astype(BF)
    for w in range(rows):
        row_ref[w * CH : (w + 1) * CH] = pred[:, w * NS : (w + 1) * NS]
    out_ref[...] = mm(row_swap_matrix(rows, CH), row_ref[...]).astype(BF)


def body(inputs, cotangent, weight_one, bias_one, weight_two, bias_two, dilation):
    rows = inputs.shape[2]
    wrap = lax.axis_size("wrap")
    pairs = lax.axis_size("x")
    group = wrap * pairs
    factor = 1.0 / math.sqrt(inputs.shape[0] * pairs * 2 * rows * wrap * NS)
    piece = -(-1737 // (2 * group * 8)) * 8
    total = 2 * group * piece
    side = total // 2
    cells = rows * NS
    ext = cells + 2 * NEAR
    first = [(i, i ^ 1) for i in range(wrap)]
    second = [(i, (i + 1) % wrap if i % 2 else (i - 1) % wrap) for i in range(wrap)]
    swap = [(0, 1), (1, 0)]
    core = lax.axis_index("core").astype(jnp.int32).reshape(1)
    parity = (lax.axis_index("wrap").astype(jnp.int32) & 1).reshape(1)

    x2 = inputs.reshape(CH * rows, NS)
    c2 = cotangent.reshape(CH * rows, NS)
    flat = sds((rows * CH, NS), BF)
    halo = sds((2 * HALF, NS), BF)
    xp, cp, send_a, send_b = call(
        lambda *refs: prep_kernel(rows, *refs),
        (flat, flat, halo, halo),
        ins=[SM, VM, VM],
        name="prep",
        mib=8,
    )(parity, x2, c2)
    got_a = lax.ppermute(send_a, "wrap", first)
    got_b = lax.ppermute(send_b, "wrap", second)

    stack = sds((TAPS, cells), BF)
    part = sds((CH, cells), F32)
    wide = sds((3 * CH, TAPS), BF)
    mats = sds((9 * NS, NS), BF)
    xs, cs, pre, back, w1, wf, m1, m2 = call(
        lambda *refs: local_kernel(rows, *refs),
        (stack, stack, part, part, wide, wide, mats, mats),
        scratch=[pltpu.VMEM((CH, ext), F32)],
        ins=[SM] + [VM] * 4,
        flops=4 * 10**9,
        nbytes=8 * 10**6,
        name="local",
    )(dilation, xp, cp, weight_one, weight_two)

    edge = sds((HALF, NS), BF)
    hid, hid_a, hid_b, keep, send = call(
        lambda *refs: grad_kernel(rows, total, factor, *refs),
        (flat, edge, edge, sds((side, 128), F32), sds((side, 128), BF)),
        scratch=[
            pltpu.VMEM((CH, ext), F32),
            pltpu.VMEM((CH, cells + 4 * NEAR), BF),
            pltpu.VMEM((3 * CH, cells), BF),
            pltpu.VMEM((TAPS, 2 * NEAR), BF),
            pltpu.VMEM((TAPS, 2 * NEAR), BF),
            pltpu.VMEM((total, 128), F32),
        ],
        ins=[SM, SM, SM] + [VM] * 11,
        flops=4 * 10**9,
        nbytes=8 * 10**6,
        name="grads",
    )(dilation, core, parity, bias_one.reshape(1, CH), got_a, got_b, w1, wf, xs, cs, pre, back, m1, m2)

    got = lax.ppermute(send, "core", swap)
    both = call(pair_kernel, sds((side, 128), BF), ins=[VM, VM], name="pair", mib=8)(keep, got)
    hid_a, hid_b, both = lax.optimization_barrier((hid_a, hid_b, both))
    with jax.named_scope("scatter"):
        parts = lax.all_to_all(both.reshape(group, piece, 128), ("wrap", "x"), 0, 0, tiled=True)
    halo_a = lax.ppermute(hid_a, "wrap", first)
    halo_b = lax.ppermute(hid_b, "wrap", second)
    guess, w2 = call(
        lambda *refs: guess_kernel(rows, *refs),
        (part, wide),
        scratch=[pltpu.VMEM((TAPS, cells), BF), pltpu.VMEM((CH, ext), F32)],
        ins=[SM, VM, VM, VM, ANY],
        flops=4 * 10**9,
        nbytes=8 * 10**6,
        name="guess",
    )(dilation, hid, weight_two, m2, both)
    mine = call(
        lambda *refs: reduce_kernel(group, *refs),
        sds((group, piece, 128), BF),
        ins=[VM, ANY],
        name="reduce",
        mib=8,
    )(parts, guess)
    with jax.named_scope("gather"):
        gathered = lax.all_to_all(mine, ("wrap", "x"), 0, 0, tiled=True).reshape(side, 128)
    other = lax.ppermute(gathered, "core", swap)
    pred = call(
        lambda *refs: predict_kernel(rows, *refs),
        flat,
        scratch=[
            pltpu.VMEM((TAPS, 2 * NEAR), BF),
            pltpu.VMEM((CH, ext), F32),
            pltpu.VMEM((rows * CH, NS), BF),
        ],
        ins=[SM, SM] + [VM] * 6,
        flops=4 * 10**9,
        nbytes=8 * 10**6,
        name="predict",
    )(dilation, parity, halo_a, halo_b, w2, bias_two.reshape(1, CH), m2, guess)
    row = sds((1, CH), F32)
    full = sds((CH, 3 * TAPS), F32)
    g1, b1, g2, b2 = call(
        lambda *refs: unpack_kernel(total, *refs),
        (full, row, full, row),
        scratch=[pltpu.VMEM((total, 128), F32)],
        ins=[SM, VM, VM],
        name="unpack",
        mib=8,
    )(core, gathered, other)
    return (pred.reshape(1, CH, rows, NS), g1, b1.reshape(CH), g2, b2.reshape(CH))


def solution(mesh):
    wrap, samp = mesh.devices.shape
    split = Mesh(mesh.devices.reshape(wrap, samp // 2, 2), ("wrap", "x", "core"))
    field = P(("x", "core"), None, "wrap", None)
    return jax.shard_map(
        body,
        mesh=split,
        in_specs=(field, field, P(), P(), P(), P(), P()),
        out_specs=(field, P(), P(), P(), P()),
        check_vma=False,
    )
```

time: 77.7 us -> 62.9 us (0.81)
  blocking collectives: 15.4 us -> 0 us
  waiting for transfers between devices: 6.76 us -> 17.2 us
  Pallas kernels: 27.9 us -> 17.7 us
  starting transfers between devices: 14.6 us -> 22.4 us
  local copies, waits for them, and re-layouts: 9.05 us -> 4.44 us
  other arithmetic: 2.77 us -> 0 us
    all_to_all x1 -> x0, blocking collectives: 15.4 us -> none  [body(): lax.all_to_all(both.reshape(group, piece, 128), ('wrap', 'x'), 0, 0, tile...]
    all_to_all x0 -> x1, waiting for transfers between devices: none -> 7.48 us  [body(): lax.all_to_all(both.reshape(group, piece, 128), ('wrap', 'x'), 0, 0, tile...]
    pallas_call x5 -> x6, Pallas kernels: 21.2 us -> 14 us  [the longest x1 6.1 us: body(): call(lambda *refs: grad_kernel(rows, total, factor, *refs), (flat, edge,...]
    all_to_all x0 -> x1, starting transfers between devices: none -> 7.08 us  [body(): lax.all_to_all(both.reshape(group, piece, 128), ('wrap', 'x'), 0, 0, tile...]
    reshape x5 -> x0, local copies, waits for them, and re-layouts: 3.16 us -> none  [the longest x1 1.41 us: body(): weight_two.reshape(CH, 27, CH)[:, ::-1, :]]
    pallas_call x2 -> x0, other arithmetic: 2.77 us -> none  [body(): call(lambda *refs: unpack_kernel(total, *refs), (sds((CH, 1728), F32), sd...]
    transpose x4 -> x0, local copies, waits for them, and re-layouts: 2.55 us -> none  [the longest x3 2.37 us: by_row_tap(): return weight.reshape(CH, 3, 576).transpose(1, 0, 2).reshape(192, 576)]
    pallas_call x1, Pallas kernels: 5 us -> 2.91 us  [body(): call(lambda *refs: predict_kernel(rows, *refs), flat, scratch=[pltpu.VMEM...]
  transfers between devices with their start and end apart: 7 -> 8, of which waited for: 4 -> 5; matrix products, arithmetic and copies ran while one was open for 8% -> 0% of each run, Pallas kernels for 13% -> 14%
where the time goes in v2:
time: 62.9 us; the launch traced here: 62.4 us
  starting transfers between devices  22.4 us (36%)
  Pallas kernels  17.7 us (28%)
  waiting for transfers between devices  17.2 us (27%)
  local copies, waits for them, and re-layouts  4.44 us (7%)
  between operations  0.74 us (1%)
    all_to_all x1, waiting for transfers between devices, body(): lax.all_to_all(both.reshape(group, piece, 128), ('wrap', 'x'), 0, 0, tile...  7.48 us
    all_to_all x1, starting transfers between devices, body(): lax.all_to_all(both.reshape(group, piece, 128), ('wrap', 'x'), 0, 0, tile...  7.08 us
    pallas_call x1, Pallas kernels, body(): call(lambda *refs: grad_kernel(rows, total, factor, *refs), (flat, edge,...  6.1 us
    all_to_all x1, waiting for transfers between devices, body(): lax.all_to_all(mine, ('wrap', 'x'), 0, 0, tiled=True).reshape(side, 128)  5.11 us
    unnamed x18, local copies, waits for them, and re-layouts  4.44 us
    pallas_call x1, Pallas kernels, body(): call(lambda *refs: local_kernel(rows, *refs), (stack, stack, part, part,...  3.55 us
    ppermute x1, starting transfers between devices, body(): got_b = lax.ppermute(send_b, 'wrap', second)  3.53 us
    all_to_all x1, starting transfers between devices, body(): lax.all_to_all(mine, ('wrap', 'x'), 0, 0, tiled=True).reshape(side, 128)  3.53 us
  transfers between devices with their start and end apart: 8, of which 5 were waited for; matrix products, arithmetic and copies ran while one was open for 0% of the time, Pallas kernels for 14%

profile of v2, /device:TPU:0, one launch (start us, length us, event | category | flops | bytes accessed | tf_op | source)
XLA Modules:
  0.0 62.4 jit_solution(6598255507887178175)
XLA Ops:
  0.6 0.0 copy-start
  0.6 0.9 %copy-done = bf16[1,64,8,256]{3,2,1,0:T(8,128)(2,1)S(1)} copy-done((bf16[1,64,8,256]{3,2,1,0:T(8,128)(2,1)S(1)}, bf16[1,64,8,256]{3,2,1,0:T(8,128)(2,1)}, u32[]{:S(2)}) %copy-start) | copy-done | bytes 262168
  1.6 0.0 copy-start.1
  1.6 0.9 %copy-done.1 = bf16[1,64,8,256]{3,2,1,0:T(8,128)(2,1)S(1)} copy-done((bf16[1,64,8,256]{3,2,1,0:T(8,128)(2,1)S(1)}, bf16[1,64,8,256]{3,2,1,0:T(8,128)(2,1)}, u32[]{:S(2)}) %copy-start.1) | copy-done | bytes 262168
  2.5 0.5 prep.1
  3.0 3.1 %collective-permute-start = (bf16[512,256]{1,0:T(8,128)(2,1)S(1)}, bf16[512,256]{1,0:T(8,128)(2,1)S(1)}, u32[]{:S(2)}, u32[]{:S(2)}) collective-permute-start(bf16[512,256]{1,0:T(8,128)(2,1)S(1)} %get-tuple-element.31), channel_id=1, source_target_pairs={{0,4},{4,0},{8,12},{12,8},{16,20},{20,16},{24,28},{28,24},{1,5},{5... | collective-permute-start | bytes 786440 | tf_op jit(solution)/shard_map/ppermute | solution.py:305
  6.1 3.5 %collective-permute-start.1 = (bf16[512,256]{1,0:T(8,128)(2,1)S(1)}, bf16[512,256]{1,0:T(8,128)(2,1)S(1)}, u32[]{:S(2)}, u32[]{:S(2)}) collective-permute-start(bf16[512,256]{1,0:T(8,128)(2,1)S(1)} %get-tuple-element.32), channel_id=1, source_target_pairs={{0,28},{4,8},{8,4},{12,16},{16,12},{20,24},{24,20},{28,0},{1,29},{... | collective-permute-start | bytes 786440 | tf_op jit(solution)/shard_map/ppermute | solution.py:306
  9.6 0.0 copy-start.2
  9.6 0.9 %copy-done.2 = bf16[64,1728]{1,0:T(8,128)(2,1)S(1)} copy-done((bf16[64,1728]{1,0:T(8,128)(2,1)S(1)}, bf16[64,1728]{1,0:T(8,128)(2,1)}, u32[]{:S(2)}) %copy-start.2) | copy-done | bytes 221208
  10.6 0.0 copy-start.3
  10.6 0.9 %copy-done.3 = bf16[64,1728]{1,0:T(8,128)(2,1)S(1)} copy-done((bf16[64,1728]{1,0:T(8,128)(2,1)S(1)}, bf16[64,1728]{1,0:T(8,128)(2,1)}, u32[]{:S(2)}) %copy-start.3) | copy-done | bytes 221208
  11.5 0.0 copy-start.6
  11.5 0.7 %copy-done.6 = s32[2]{0:T(128)S(1)} copy-done((s32[2]{0:T(128)S(1)}, s32[2]{0:T(128)}, u32[]{:S(2)}) %copy-start.6) | copy-done | bytes 32
  12.2 0.0 copy-start.5
  12.2 0.0 copy-start.7
  12.2 3.5 %local.1 = (bf16[576,2048]{1,0:T(8,128)(2,1)S(1)}, bf16[576,2048]{1,0:T(8,128)(2,1)S(1)}, f32[64,2048]{1,0:T(8,128)S(1)}, f32[64,2048]{1,0:T(8,128)S(1)}, bf16[1...) custom-call(s32[2]{0:T(128)S(1)} %copy-done.6, ...), custom_call_target="tpu_custom_call" | custom-call | flops 4000000000 | bytes 8000000 | tf_op jit(solution)/shard_map/local/pallas_call | solution.py:312
  15.7 2.3 %collective-permute-done.refs_4_ = bf16[512,256]{1,0:T(8,128)(2,1)S(1)} collective-permute-done((bf16[512,256]{1,0:T(8,128)(2,1)S(1)}, bf16[512,256]{1,0:T(8,128)(2,1)S(1)}, u32[]{:S(2)}, u32[]{:S(2)}) %collective-permute-start) | collective-permute-done | bytes 262176 | tf_op jit(solution)/shard_map/ppermute | solution.py:305
  18.0 0.0 collective-permute-done.1.refs_5_
  18.0 0.0 copy-done.5
  18.0 0.0 copy-done.7
  18.0 0.0 copy-start.4
  18.0 6.1 %grads.1 = (bf16[512,256]{1,0:T(8,128)(2,1)S(1)}, bf16[256,256]{1,0:T(8,128)(2,1)S(1)}, bf16[256,256]{1,0:T(8,128)(2,1)S(1)}, f32[896,128]{1,0:T(8,128)S(1)}, bf16[896,128]{1,0:T(8,128)(2,1)S(1)}) custom-call(s32[2]{0:T(128)S(1)} %copy-done.7, s32[1]{0:T(128)} %bitcast.1.refs_1_.refs_0_, s32[1]{0:T(128)} %bitcast.refs_0_.refs_2_.refs_1_, ...), custom_call_target="tpu_custom_call" | custom-call | flops 4000000000 | bytes 8000000 | tf_op jit(solution)/shard_map/grads/pallas_call | solution.py:323
  24.1 0.1 collective-permute-start.2
  24.2 1.5 %collective-permute-done.2.got_ref = bf16[896,128]{1,0:T(8,128)(2,1)S(1)} collective-permute-done((bf16[896,128]{1,0:T(8,128)(2,1)S(1)}, bf16[896,128]{1,0:T(8,128)(2,1)S(1)}, u32[]{:S(2)}, u32[]{:S(2)}) %collective-permute-start.2) | collective-permute-done | bytes 229408 | tf_op jit(solution)/shard_map/ppermute | solution.py:340
  25.7 0.7 %pair.1.refs_4_ = bf16[896,128]{1,0:T(8,128)(2,1)} custom-call(f32[896,128]{1,0:T(8,128)S(1)} %get-tuple-element.45.keep_ref, bf16[896,128]{1,0:T(8,128)(2,1)S(1)} %collective-permute-done.2.got_ref), custom_call_target="tpu_custom_call" | custom-call | flops 100000000 | bytes 1000000 | tf_op jit(solution)/shard_map/pair/pallas_call | solution.py:341
  26.4 7.1 %all-to-all-start = ((bf16[16,56,128]{2,1,0:T(8,128)(2,1)}), bf16[16,56,128]{2,1,0:T(8,128)(2,1)S(1)}, u32[]{:S(2)}, u32[]{:S(2)}) async-start(bf16[16,56,128]{2,1,0:T(8,128)(2,1)} %bitcast.7), calls=%async_computation | async-start | bytes 458752 | tf_op jit(solution)/shard_map/scatter/all_to_all | solution.py:344
  33.5 0.0 copy-done.4
  33.5 0.0 copy-start.8
  33.5 2.0 %guess.1 = (f32[64,2048]{1,0:T(8,128)S(1)}, bf16[192,576]{1,0:T(8,128)(2,1)S(1)}) custom-call(s32[2]{0:T(128)S(1)} %copy-done.7, bf16[512,256]{1,0:T(8,128)(2,1)S(1)} %get-tuple-element.49.refs_1_, bf16[64,1728]{1,0:T(8,128)(2,1)S(1)} %copy-done.4, bf16[2304,256]{1,0:T(8,128)(2,1)S(1)} %get-tuple-element.42.refs_13_.refs_3_.refs_6_, ...), custom_call_target="tpu_custom_call" | custom-call | flops 4000000000 | bytes 8000000 | tf_op jit(solution)/shard_map/guess/pallas_call | solution.py:347
  35.6 7.5 %all-to-all-done.refs_0_ = bf16[16,56,128]{2,1,0:T(8,128)(2,1)S(1)} async-done(((bf16[16,56,128]{2,1,0:T(8,128)(2,1)}), bf16[16,56,128]{2,1,0:T(8,128)(2,1)S(1)}, u32[]{:S(2)}, u32[]{:S(2)}) %all-to-all-start) | async-done | bytes 229408 | tf_op jit(solution)/shard_map/scatter/all_to_all | solution.py:344
  43.1 0.7 %reduce.1 = bf16[16,56,128]{2,1,0:T(8,128)(2,1)} custom-call(bf16[16,56,128]{2,1,0:T(8,128)(2,1)S(1)} %all-to-all-done.refs_0_, f32[64,2048]{1,0:T(8,128)S(1)} %get-tuple-element.52.refs_7_.refs_1_), custom_call_target="tpu_custom_call" | custom-call | flops 100000000 | bytes 1000000 | tf_op jit(solution)/shard_map/reduce/pallas_call | solution.py:356
  43.8 3.5 %all-to-all-start.1 = ((bf16[16,56,128]{2,1,0:T(8,128)(2,1)}), bf16[16,56,128]{2,1,0:T(8,128)(2,1)S(1)}, u32[]{:S(2)}, u32[]{:S(2)}) async-start(bf16[16,56,128]{2,1,0:T(8,128)(2,1)} %reduce.1), calls=%async_computation.1 | async-start | bytes 458752 | tf_op jit(solution)/shard_map/gather/all_to_all | solution.py:364
  47.3 1.9 %collective-permute-start.3 = (bf16[256,256]{1,0:T(8,128)(2,1)S(1)}, bf16[256,256]{1,0:T(8,128)(2,1)S(1)}, u32[]{:S(2)}, u32[]{:S(2)}) collective-permute-start(bf16[256,256]{1,0:T(8,128)(2,1)S(1)} %get-tuple-element.47), channel_id=1, source_target_pairs={{0,4},{4,0},{8,12},{12,8},{16,20},{20,16},{24,28},{28,24},{1,5},{5... | collective-permute-start | bytes 393224 | tf_op jit(solution)/shard_map/ppermute | solution.py:345
  49.2 3.3 %collective-permute-start.4 = (bf16[256,256]{1,0:T(8,128)(2,1)S(1)}, bf16[256,256]{1,0:T(8,128)(2,1)S(1)}, u32[]{:S(2)}, u32[]{:S(2)}) collective-permute-start(bf16[256,256]{1,0:T(8,128)(2,1)S(1)} %get-tuple-element.48), channel_id=1, source_target_pairs={{0,28},{4,8},{8,4},{12,16},{16,12},{20,24},{24,20},{28,0},{1,29},{... | collective-permute-start | bytes 393224 | tf_op jit(solution)/shard_map/ppermute | solution.py:346
  52.5 5.1 %all-to-all-done.1 = bf16[16,56,128]{2,1,0:T(8,128)(2,1)S(1)} async-done(((bf16[16,56,128]{2,1,0:T(8,128)(2,1)}), bf16[16,56,128]{2,1,0:T(8,128)(2,1)S(1)}, u32[]{:S(2)}, u32[]{:S(2)}) %all-to-all-start.1) | async-done | bytes 229408 | tf_op jit(solution)/shard_map/gather/all_to_all | solution.py:364
  57.6 0.0 collective-permute-start.5
  57.6 0.0 collective-permute-done.3.refs_2_
  57.6 0.8 %collective-permute-done.4.refs_3_ = bf16[256,256]{1,0:T(8,128)(2,1)S(1)} collective-permute-done((bf16[256,256]{1,0:T(8,128)(2,1)S(1)}, bf16[256,256]{1,0:T(8,128)(2,1)S(1)}, u32[]{:S(2)}, u32[]{:S(2)}) %collective-permute-start.4) | collective-permute-done | bytes 131104 | tf_op jit(solution)/shard_map/ppermute | solution.py:346
  58.4 0.0 copy-done.8
  58.4 2.9 %predict.1 = bf16[512,256]{1,0:T(8,128)(2,1)} custom-call(s32[2]{0:T(128)S(1)} %copy-done.7, s32[1]{0:T(128)} %bitcast.refs_0_.refs_2_.refs_1_, bf16[256,256]{1,0:T(8,128)(2,1)S(1)} %collective-permute-done.3.refs_2_, bf16[256,256]{1,0:T(8,128)(2,1)S(1)} %collective-permute-done.4.refs_3_, bf16[192,576]{1,0:T(8,128)(2,1)S(1)} %get-tuple-element.51.refs_4_, ...), custom_call_target="tpu_custom_call" | custom-call | flops 4000000000 | bytes 8000000 | tf_op jit(solution)/shard_map/predict/pallas_call | solution.py:366
  61.3 0.0 collective-permute-done.5.refs_2_
  61.3 1.1 %unpack.1 = (f32[64,1728]{1,0:T(8,128)}, f32[1,64]{1,0:T(1,128)}, f32[64,1728]{1,0:T(8,128)}, f32[1,64]{1,0:T(1,128)}) custom-call(s32[1]{0:T(128)} %bitcast.1.refs_1_.refs_0_, bf16[896,128]{1,0:T(8,128)(2,1)S(1)} %bitcast.12, bf16[896,128]{1,0:T(8,128)(2,1)S(1)} %collective-permute-done.5.refs_2_), custom_call_target="tpu_custom_call" | custom-call | flops 100000000 | bytes 1000000 | tf_op jit(solution)/shard_map/unpack/pallas_call | solution.py:381
Async XLA Ops:
  0.6 1.0 %copy-start = (bf16[1,64,8,256]{3,2,1,0:T(8,128)(2,1)S(1)}, bf16[1,64,8,256]{3,2,1,0:T(8,128)(2,1)}, u32[]{:S(2)}) copy-start(bf16[1,64,8,256]{3,2,1,0:T(8,128)(2,1)} %param.7) | copy-start | bytes 786436
  1.6 0.9 %copy-start.1 = (bf16[1,64,8,256]{3,2,1,0:T(8,128)(2,1)S(1)}, bf16[1,64,8,256]{3,2,1,0:T(8,128)(2,1)}, u32[]{:S(2)}) copy-start(bf16[1,64,8,256]{3,2,1,0:T(8,128)(2,1)} %param.8) | copy-start | bytes 786436
  3.0 15.0 %collective-permute-start = (bf16[512,256]{1,0:T(8,128)(2,1)S(1)}, bf16[512,256]{1,0:T(8,128)(2,1)S(1)}, u32[]{:S(2)}, u32[]{:S(2)}) collective-permute-start(bf16[512,256]{1,0:T(8,128)(2,1)S(1)} %get-tuple-element.31), channel_id=1, source_target_pairs={{0,4},{4,0},{8,12},{12,8},{16,20},{20,16},{24,28},{28,24},{1,5},{5... | collective-permute-start | bytes 786440 | tf_op jit(solution)/shard_map/ppermute | solution.py:305
  6.1 11.9 %collective-permute-start.1 = (bf16[512,256]{1,0:T(8,128)(2,1)S(1)}, bf16[512,256]{1,0:T(8,128)(2,1)S(1)}, u32[]{:S(2)}, u32[]{:S(2)}) collective-permute-start(bf16[512,256]{1,0:T(8,128)(2,1)S(1)} %get-tuple-element.32), channel_id=1, source_target_pairs={{0,28},{4,8},{8,4},{12,16},{16,12},{20,24},{24,20},{28,0},{1,29},{... | collective-permute-start | bytes 786440 | tf_op jit(solution)/shard_map/ppermute | solution.py:306
  9.6 0.9 %copy-start.2 = (bf16[64,1728]{1,0:T(8,128)(2,1)S(1)}, bf16[64,1728]{1,0:T(8,128)(2,1)}, u32[]{:S(2)}) copy-start(bf16[64,1728]{1,0:T(8,128)(2,1)} %refs_3_.1) | copy-start | bytes 663556
  10.6 0.9 %copy-start.3 = (bf16[64,1728]{1,0:T(8,128)(2,1)S(1)}, bf16[64,1728]{1,0:T(8,128)(2,1)}, u32[]{:S(2)}) copy-start(bf16[64,1728]{1,0:T(8,128)(2,1)} %refs_2_.1) | copy-start | bytes 663556
  11.5 0.7 %copy-start.6 = (s32[2]{0:T(128)S(1)}, s32[2]{0:T(128)}, u32[]{:S(2)}) copy-start(s32[2]{0:T(128)} %refs_0_.7) | copy-start | bytes 28
  12.2 5.9 %copy-start.5 = (f32[64]{0:T(128)S(1)}, f32[64]{0:T(128)}, u32[]{:S(2)}) copy-start(f32[64]{0:T(128)} %param.10) | copy-start | bytes 772
  12.2 5.9 %copy-start.7 = (s32[2]{0:T(128)S(1)}, s32[2]{0:T(128)}, u32[]{:S(2)}) copy-start(s32[2]{0:T(128)} %refs_0_.7) | copy-start | bytes 28
  18.0 15.5 %copy-start.4 = (bf16[64,1728]{1,0:T(8,128)(2,1)S(1)}, bf16[64,1728]{1,0:T(8,128)(2,1)}, u32[]{:S(2)}) copy-start(bf16[64,1728]{1,0:T(8,128)(2,1)} %refs_2_.1) | copy-start | bytes 663556
  24.1 1.6 %collective-permute-start.2 = (bf16[896,128]{1,0:T(8,128)(2,1)S(1)}, bf16[896,128]{1,0:T(8,128)(2,1)S(1)}, u32[]{:S(2)}, u32[]{:S(2)}) collective-permute-start(bf16[896,128]{1,0:T(8,128)(2,1)S(1)} %get-tuple-element.46), channel_id=1, source_target_pairs={{0,1},{1,0},{2,3},{3,2},{4,5},{5,4},{6,7},{7,6},{8,9},{9,8},{10,11... | collective-permute-start | bytes 688136 | tf_op jit(solution)/shard_map/ppermute | solution.py:340
  26.4 16.6 %all-to-all-start = ((bf16[16,56,128]{2,1,0:T(8,128)(2,1)}), bf16[16,56,128]{2,1,0:T(8,128)(2,1)S(1)}, u32[]{:S(2)}, u32[]{:S(2)}) async-start(bf16[16,56,128]{2,1,0:T(8,128)(2,1)} %bitcast.7), calls=%async_computation | async-start | bytes 458752 | tf_op jit(solution)/shard_map/scatter/all_to_all | solution.py:344
  33.5 24.9 %copy-start.8 = (f32[64]{0:T(128)S(1)}, f32[64]{0:T(128)}, u32[]{:S(2)}) copy-start(f32[64]{0:T(128)} %param.12) | copy-start | bytes 772
  43.8 13.8 %all-to-all-start.1 = ((bf16[16,56,128]{2,1,0:T(8,128)(2,1)}), bf16[16,56,128]{2,1,0:T(8,128)(2,1)S(1)}, u32[]{:S(2)}, u32[]{:S(2)}) async-start(bf16[16,56,128]{2,1,0:T(8,128)(2,1)} %reduce.1), calls=%async_computation.1 | async-start | bytes 458752 | tf_op jit(solution)/shard_map/gather/all_to_all | solution.py:364
  47.3 10.3 %collective-permute-start.3 = (bf16[256,256]{1,0:T(8,128)(2,1)S(1)}, bf16[256,256]{1,0:T(8,128)(2,1)S(1)}, u32[]{:S(2)}, u32[]{:S(2)}) collective-permute-start(bf16[256,256]{1,0:T(8,128)(2,1)S(1)} %get-tuple-element.47), channel_id=1, source_target_pairs={{0,4},{4,0},{8,12},{12,8},{16,20},{20,16},{24,28},{28,24},{1,5},{5... | collective-permute-start | bytes 393224 | tf_op jit(solution)/shard_map/ppermute | solution.py:345
  49.2 9.2 %collective-permute-start.4 = (bf16[256,256]{1,0:T(8,128)(2,1)S(1)}, bf16[256,256]{1,0:T(8,128)(2,1)S(1)}, u32[]{:S(2)}, u32[]{:S(2)}) collective-permute-start(bf16[256,256]{1,0:T(8,128)(2,1)S(1)} %get-tuple-element.48), channel_id=1, source_target_pairs={{0,28},{4,8},{8,4},{12,16},{16,12},{20,24},{24,20},{28,0},{1,29},{... | collective-permute-start | bytes 393224 | tf_op jit(solution)/shard_map/ppermute | solution.py:346
  57.6 3.7 %collective-permute-start.5 = (bf16[896,128]{1,0:T(8,128)(2,1)S(1)}, bf16[896,128]{1,0:T(8,128)(2,1)S(1)}, u32[]{:S(2)}, u32[]{:S(2)}) collective-permute-start(bf16[896,128]{1,0:T(8,128)(2,1)S(1)} %bitcast.11), channel_id=1, source_target_pairs={{0,1},{1,0},{2,3},{3,2},{4,5},{5,4},{6,7},{7,6},{8,9},{9,8},{10,11... | collective-permute-start | bytes 688136 | tf_op jit(solution)/shard_map/ppermute | solution.py:365

commit v3 on v2

--- a/solution.py
+++ b/solution.py
@@ -7,6 +7,7 @@
 from jax.experimental.pallas import tpu as pltpu
 from jax.sharding import Mesh
 from jax.sharding import PartitionSpec as P
+
 
 DMAX = 4
 NR = 16
@@ -21,14 +22,14 @@
 
 VM = pl.BlockSpec(memory_space=pltpu.VMEM)
 SM = pl.BlockSpec(memory_space=pltpu.SMEM)
-ANY = pl.BlockSpec(memory_space=pl.ANY)
+HBM = pl.BlockSpec(memory_space=pltpu.HBM)
 
 
 def sds(shape, dtype):
     return jax.ShapeDtypeStruct(shape, dtype)
 
 
-def call(kernel, outs, scratch=(), ins=None, flops=10**8, nbytes=10**6, name=None, mib=24):
+def call(kernel, outs, scratch=(), ins=None, flops=10**8, nbytes=10**6, mib=16):
     return pl.pallas_call(
         kernel,
         out_shape=outs,
@@ -37,7 +38,6 @@
         scratch_shapes=list(scratch),
         cost_estimate=pl.CostEstimate(flops=flops, bytes_accessed=nbytes, transcendentals=0),
         compiler_params=pltpu.CompilerParams(vmem_limit_bytes=mib * 1024 * 1024),
-        name=name,
     )
 
 
@@ -90,13 +90,17 @@
     return jnp.sum(jnp.where(i == j, jnp.broadcast_to(row, (CH, CH)), 0.0), 1, keepdims=True)
 
 
-def prep_kernel(rows, par_ref, x_ref, c_ref, xp_ref, cp_ref, a_ref, b_ref):
+def prep_kernel(rows, par_ref, core_ref, x_hbm, c_hbm, xp_ref, cp_ref, a_ref, b_ref, x_ref, c_ref, sem):
+    copies = [pltpu.make_async_copy(x_hbm, x_ref, sem.at[0]), pltpu.make_async_copy(c_hbm, c_ref, sem.at[1])]
+    for copy in copies:
+        copy.start()
     even = par_ref[0] == 0
     last = rows * CH - HALF
     first_at = pl.ds(pl.multiple_of(jnp.where(even, last, 0), CH), HALF)
     second_at = pl.ds(pl.multiple_of(jnp.where(even, 0, last), CH), HALF)
     perm = row_swap_matrix(CH, rows)
     for k, (src, dst) in enumerate(((x_ref, xp_ref), (c_ref, cp_ref))):
+        copies[k].wait()
         dst[...] = mm(perm, src[...]).astype(BF)
         a_ref[k * HALF : (k + 1) * HALF] = dst[first_at]
         b_ref[k * HALF : (k + 1) * HALF] = dst[second_at]
@@ -130,16 +134,44 @@
 
 def local_kernel(
     rows,
-    d_ref, xp_ref, cp_ref, one_ref, two_ref,
+    d_ref, xp_ref, cp_ref, one_hbm, two_hbm,
     xs_ref, cs_ref, pre_ref, back_ref, w1_ref, wf_ref, m1_ref, m2_ref,
+    pad_ref, one_ref, two_ref, sem,
+):
+    copies = [pltpu.make_async_copy(one_hbm, one_ref, sem.at[0]), pltpu.make_async_copy(two_hbm, two_ref, sem.at[1])]
+    for copy in copies:
+        copy.start()
+    shift_matrices(d_ref[0], m1_ref)
+    shift_matrices(d_ref[1], m2_ref)
+    copies[0].wait()
+    rows_by_tap(one_ref, w1_ref)
+    local_part(rows, xp_ref[...], d_ref[0], w1_ref, m1_ref, xs_ref, pre_ref, pad_ref)
+    copies[1].wait()
+    flipped_rows(two_ref, wf_ref)
+    local_part(rows, cp_ref[...], d_ref[1], wf_ref, m2_ref, cs_ref, back_ref, pad_ref)
+
+
+def side_part(rows, before, cells, rate, w_ref, mats_ref, stack_ref, part, pad_ref):
+    shifted(cells, mats_ref, stack_ref)
+    pad_ref[:, NEAR : NEAR + rows * NS] = part
+    weight = w_ref[pl.ds(pl.multiple_of(jnp.where(before, 0, 2 * CH), CH), CH)]
+    pad_ref[:, lanes(jnp.where(before, rate, DMAX + rows - rate), DMAX)] += mm(weight, stack_ref[...])
+    return pad_ref[:, NEAR : NEAR + rows * NS]
+
+
+def near_kernel(
+    rows,
+    d_ref, par_ref, a_ref, w1_ref, wf_ref, m1_ref, m2_ref, pre_ref, back_ref,
+    xa_ref, ca_ref, pre_out, back_out,
     pad_ref,
 ):
-    shift_matrices(d_ref[0], m1_ref)
-    shift_matrices(d_ref[1], m2_ref)
-    rows_by_tap(one_ref, w1_ref)
-    flipped_rows(two_ref, wf_ref)
-    local_part(rows, xp_ref[...], d_ref[0], w1_ref, m1_ref, xs_ref, pre_ref, pad_ref)
-    local_part(rows, cp_ref[...], d_ref[1], wf_ref, m2_ref, cs_ref, back_ref, pad_ref)
+    before = par_ref[0] != 0
+    pre_out[...] = side_part(
+        rows, before, a_ref[:HALF], d_ref[0], w1_ref, m1_ref, xa_ref, pre_ref[...], pad_ref
+    )
+    back_out[...] = side_part(
+        rows, before, a_ref[HALF:], d_ref[1], wf_ref, m2_ref, ca_ref, back_ref[...], pad_ref
+    )
 
 
 def halo_part(rows, before, after, rate, w_ref, mats_ref, stack_ref, part, pad_ref):
@@ -158,24 +190,25 @@
     out_ref[:CH] = pad_ref[:, lanes(2 * DMAX + rate, rows)]
     out_ref[CH : 2 * CH] = value
     out_ref[2 * CH :] = pad_ref[:, lanes(2 * DMAX - rate, rows)]
-    return pad_ref[:, lanes(DMAX + rate, DMAX)], pad_ref[:, lanes(2 * DMAX + rows - rate, DMAX)]
+    def side(before):
+        return pad_ref[:, lanes(jnp.where(before, DMAX + rate, 2 * DMAX + rows - rate), DMAX)]
+
+    return side
 
 
 def grad_kernel(
     rows, total, factor,
-    d_ref, core_ref, par_ref, b1_ref, a_ref, b_ref, w1_ref, wf_ref, xs_ref, cs_ref, pre_ref, back_ref, m1_ref, m2_ref,
+    d_ref, core_ref, par_ref, b1_ref, b_ref, w1_ref, wf_ref, xs_ref, cs_ref, xa_ref, ca_ref, pre_ref, back_ref,
+    m1_ref, m2_ref,
     hid_ref, ha_ref, hb_ref, keep_ref, send_ref,
-    pad_ref, pad16_ref, tri_ref, xh_ref, ch_ref, all_ref,
+    pad_ref, pad16_ref, tri_ref, xb_ref, cb_ref, all_ref,
 ):
     r1 = d_ref[0]
     r2 = d_ref[1]
     even = par_ref[0] == 0
+    odd = par_ref[0] != 0
     cells = rows * NS
-    one = a_ref[...]
-    two = b_ref[...]
-    up = jnp.where(even, two, one)
-    down = jnp.where(even, one, two)
-    pre = halo_part(rows, up[:HALF], down[:HALF], r1, w1_ref, m1_ref, xh_ref, pre_ref[...], pad_ref)
+    pre = side_part(rows, even, b_ref[:HALF], r1, w1_ref, m1_ref, xb_ref, pre_ref[...], pad_ref)
     pre = pre + column(b1_ref[...])
     sigm = 1.0 / (1.0 + jnp.exp(-pre))
     hidden = (pre * sigm).astype(BF)
@@ -185,21 +218,25 @@
     ha_ref[...] = hid_ref[pl.ds(pl.multiple_of(jnp.where(even, last, 0), CH), HALF)]
     hb_ref[...] = hid_ref[pl.ds(pl.multiple_of(jnp.where(even, 0, last), CH), HALF)]
     slope = sigm * (1.0 + pre * (1.0 - sigm))
-    back = halo_part(rows, up[HALF:], down[HALF:], r2, wf_ref, m2_ref, ch_ref, back_ref[...], pad_ref)
+    back = side_part(rows, even, b_ref[HALF:], r2, wf_ref, m2_ref, cb_ref, back_ref[...], pad_ref)
     back_pre = (back * slope).astype(BF)
 
-    before, after = triple(rows, hidden, r2, pad16_ref, tri_ref)
+    side = triple(rows, hidden, r2, pad16_ref, tri_ref)
     g2 = nt(cs_ref[...], tri_ref[...])
-    g2a = nt(ch_ref[:, :NEAR], before)
-    g2b = nt(ch_ref[:, NEAR:], after)
-    all_ref[:TAPS] = jnp.concatenate([g2[:, :CH] + g2a, g2[:, CH : 2 * CH]], 1) * factor
-    left2 = (g2[:, 2 * CH :] + g2b) * factor
-
-    before, after = triple(rows, back_pre, r1, pad16_ref, tri_ref)
+    g2a = nt(ca_ref[...], side(odd))
+    g2b = nt(cb_ref[...], side(even))
+    low = jnp.where(even, g2b, g2a)
+    high = jnp.where(even, g2a, g2b)
+    all_ref[:TAPS] = jnp.concatenate([g2[:, :CH] + low, g2[:, CH : 2 * CH]], 1) * factor
+    left2 = (g2[:, 2 * CH :] + high) * factor
+
+    side = triple(rows, back_pre, r1, pad16_ref, tri_ref)
     g1 = nt(tri_ref[...], xs_ref[...])
-    g1a = nt(before, xh_ref[:, :NEAR])
-    g1b = nt(after, xh_ref[:, NEAR:])
-    g1 = jnp.concatenate([g1[:CH] + g1a, g1[CH : 2 * CH], g1[2 * CH :] + g1b], 0) * factor
+    g1a = nt(side(odd), xa_ref[...])
+    g1b = nt(side(even), xb_ref[...])
+    low = jnp.where(even, g1b, g1a)
+    high = jnp.where(even, g1a, g1b)
+    g1 = jnp.concatenate([g1[:CH] + low, g1[CH : 2 * CH], g1[2 * CH :] + high], 0) * factor
     for k in range(4):
         all_ref[576 + 192 * k : 768 + 192 * k] = g1[:, 128 * k : 128 * (k + 1)]
     right = jnp.concatenate([left2[384:], g1[:, 512:]], 0)
@@ -218,7 +255,7 @@
     out_ref[...] = (keep_ref[...] + got_ref[...].astype(F32)).astype(BF)
 
 
-def reduce_kernel(parts, got_ref, order_ref, out_ref):
+def reduce_kernel(parts, got_ref, out_ref):
     total = got_ref[0].astype(F32)
     for k in range(1, parts):
         total = total + got_ref[k].astype(F32)
@@ -254,7 +291,10 @@
     b2_ref[...] = all_ref[1728:1729, CH:]
 
 
-def guess_kernel(rows, d_ref, hid_ref, two_ref, m2_ref, order_ref, part_ref, w2_ref, stack_ref, pad_ref):
+def guess_kernel(rows, d_ref, hid_ref, two_hbm, m2_ref, part_ref, w2_ref, stack_ref, pad_ref, two_ref, sem):
+    copy = pltpu.make_async_copy(two_hbm, two_ref, sem)
+    copy.start()
+    copy.wait()
     rows_by_tap(two_ref, w2_ref)
     local_part(rows, hid_ref[...], d_ref[1], w2_ref, m2_ref, stack_ref, part_ref, pad_ref)
 
@@ -298,10 +338,10 @@
     xp, cp, send_a, send_b = call(
         lambda *refs: prep_kernel(rows, *refs),
         (flat, flat, halo, halo),
-        ins=[SM, VM, VM],
-        name="prep",
+        scratch=[pltpu.VMEM((rows * CH, NS), BF), pltpu.VMEM((rows * CH, NS), BF), pltpu.SemaphoreType.DMA((2,))],
+        ins=[SM, SM, HBM, HBM],
         mib=8,
-    )(parity, x2, c2)
+    )(parity, core, x2, c2)
     got_a = lax.ppermute(send_a, "wrap", first)
     got_b = lax.ppermute(send_b, "wrap", second)
 
@@ -312,12 +352,28 @@
     xs, cs, pre, back, w1, wf, m1, m2 = call(
         lambda *refs: local_kernel(rows, *refs),
         (stack, stack, part, part, wide, wide, mats, mats),
-        scratch=[pltpu.VMEM((CH, ext), F32)],
-        ins=[SM] + [VM] * 4,
+        scratch=[
+            pltpu.VMEM((CH, ext), F32),
+            pltpu.VMEM((CH, 3 * TAPS), BF),
+            pltpu.VMEM((CH, 3 * TAPS), BF),
+            pltpu.SemaphoreType.DMA((2,)),
+        ],
+        ins=[SM, VM, VM, HBM, HBM],
         flops=4 * 10**9,
         nbytes=8 * 10**6,
-        name="local",
+        mib=14,
     )(dilation, xp, cp, weight_one, weight_two)
+
+    beside = sds((TAPS, NEAR), BF)
+    xa, ca, pre, back = call(
+        lambda *refs: near_kernel(rows, *refs),
+        (beside, beside, part, part),
+        scratch=[pltpu.VMEM((CH, ext), F32)],
+        ins=[SM, SM] + [VM] * 7,
+        flops=2 * 10**9,
+        nbytes=4 * 10**6,
+        mib=10,
+    )(dilation, parity, got_a, w1, wf, m1, m2, pre, back)
 
     edge = sds((HALF, NS), BF)
     hid, hid_a, hid_b, keep, send = call(
@@ -327,41 +383,37 @@
             pltpu.VMEM((CH, ext), F32),
             pltpu.VMEM((CH, cells + 4 * NEAR), BF),
             pltpu.VMEM((3 * CH, cells), BF),
-            pltpu.VMEM((TAPS, 2 * NEAR), BF),
-            pltpu.VMEM((TAPS, 2 * NEAR), BF),
+            pltpu.VMEM((TAPS, NEAR), BF),
+            pltpu.VMEM((TAPS, NEAR), BF),
             pltpu.VMEM((total, 128), F32),
         ],
-        ins=[SM, SM, SM] + [VM] * 11,
+        ins=[SM, SM, SM] + [VM] * 12,
         flops=4 * 10**9,
         nbytes=8 * 10**6,
-        name="grads",
-    )(dilation, core, parity, bias_one.reshape(1, CH), got_a, got_b, w1, wf, xs, cs, pre, back, m1, m2)
+        mib=14,
+    )(dilation, core, parity, bias_one.reshape(1, CH), got_b, w1, wf, xs, cs, xa, ca, pre, back, m1, m2)
 
     got = lax.ppermute(send, "core", swap)
-    both = call(pair_kernel, sds((side, 128), BF), ins=[VM, VM], name="pair", mib=8)(keep, got)
-    hid_a, hid_b, both = lax.optimization_barrier((hid_a, hid_b, both))
-    with jax.named_scope("scatter"):
-        parts = lax.all_to_all(both.reshape(group, piece, 128), ("wrap", "x"), 0, 0, tiled=True)
+    both = call(pair_kernel, sds((side, 128), BF), ins=[VM, VM], mib=8)(keep, got)
+    parts = lax.all_to_all(both.reshape(group, piece, 128), ("wrap", "x"), 0, 0, tiled=True)
     halo_a = lax.ppermute(hid_a, "wrap", first)
     halo_b = lax.ppermute(hid_b, "wrap", second)
     guess, w2 = call(
         lambda *refs: guess_kernel(rows, *refs),
         (part, wide),
-        scratch=[pltpu.VMEM((TAPS, cells), BF), pltpu.VMEM((CH, ext), F32)],
-        ins=[SM, VM, VM, VM, ANY],
+        scratch=[
+            pltpu.VMEM((TAPS, cells), BF),
+            pltpu.VMEM((CH, ext), F32),
+            pltpu.VMEM((CH, 3 * TAPS), BF),
+            pltpu.SemaphoreType.DMA,
+        ],
+        ins=[SM, VM, HBM, VM],
         flops=4 * 10**9,
         nbytes=8 * 10**6,
-        name="guess",
-    )(dilation, hid, weight_two, m2, both)
-    mine = call(
-        lambda *refs: reduce_kernel(group, *refs),
-        sds((group, piece, 128), BF),
-        ins=[VM, ANY],
-        name="reduce",
-        mib=8,
-    )(parts, guess)
-    with jax.named_scope("gather"):
-        gathered = lax.all_to_all(mine, ("wrap", "x"), 0, 0, tiled=True).reshape(side, 128)
+        mib=10,
+    )(dilation, hid, weight_two, m2)
+    mine = call(lambda *refs: reduce_kernel(group, *refs), sds((group, piece, 128), BF), ins=[VM], mib=8)(parts)
+    gathered = lax.all_to_all(mine, ("wrap", "x"), 0, 0, tiled=True).reshape(side, 128)
     other = lax.ppermute(gathered, "core", swap)
     pred = call(
         lambda *refs: predict_kernel(rows, *refs),
@@ -374,7 +426,7 @@
         ins=[SM, SM] + [VM] * 6,
         flops=4 * 10**9,
         nbytes=8 * 10**6,
-        name="predict",
+        mib=8,
     )(dilation, parity, halo_a, halo_b, w2, bias_two.reshape(1, CH), m2, guess)
     row = sds((1, CH), F32)
     full = sds((CH, 3 * TAPS), F32)
@@ -383,7 +435,6 @@
         (full, row, full, row),
         scratch=[pltpu.VMEM((total, 128), F32)],
         ins=[SM, VM, VM],
-        name="unpack",
         mib=8,
     )(core, gathered, other)
     return (pred.reshape(1, CH, rows, NS), g1, b1.reshape(CH), g2, b2.reshape(CH))

time: 62.9 us -> 63.4 us (level)
  blocking collectives: 0 us -> 13.5 us
  starting transfers between devices: 22.4 us -> 14.9 us
  waiting for transfers between devices: 17.2 us -> 9.87 us
  Pallas kernels: 17.7 us -> 19.5 us
    all_to_all x0 -> x1, blocking collectives: none -> 13.5 us  [body(): lax.all_to_all(both.reshape(group, piece, 128), ('wrap', 'x'), 0, 0, tile...]
    all_to_all x1 -> x0, waiting for transfers between devices: 7.48 us -> none  [body(): lax.all_to_all(both.reshape(group, piece, 128), ('wrap', 'x'), 0, 0, tile...]
    all_to_all x1 -> x0, starting transfers between devices: 7.08 us -> none  [body(): lax.all_to_all(both.reshape(group, piece, 128), ('wrap', 'x'), 0, 0, tile...]
    ppermute x1, starting transfers between devices: 3.07 us -> 0.01 us  [body(): got_a = lax.ppermute(send_a, 'wrap', first)]
    ppermute x1, waiting for transfers between devices: 2.29 us -> 4.87 us  [body(): got_a = lax.ppermute(send_a, 'wrap', first)]
    ppermute x1, starting transfers between devices: 3.53 us -> 6.08 us  [body(): got_b = lax.ppermute(send_b, 'wrap', second)]
    all_to_all x1, waiting for transfers between devices: 5.11 us -> 2.74 us  [body(): lax.all_to_all(mine, ('wrap', 'x'), 0, 0, tiled=True).reshape(side, 128)]
    pallas_call x2 -> x3, Pallas kernels: 1.21 us -> 2.98 us  [the longest x1 1.81 us: body(): call(lambda *refs: near_kernel(rows, *refs), (beside, beside, part, part)...]
  transfers between devices with their start and end apart: 8 -> 7, of which waited for: 5 -> 4; matrix products, arithmetic and copies ran while one was open for 0% -> 0% of each run, Pallas kernels for 14% -> 18%
where the time goes in v3:
time: 63.4 us; the launch traced here: 63 us
  Pallas kernels  19.5 us (31%)
  starting transfers between devices  14.9 us (24%)
  blocking collectives  13.5 us (21%)
  waiting for transfers between devices  9.87 us (16%)
  local copies, waits for them, and re-layouts  4.44 us (7%)
  between operations  0.74 us (1%)
    all_to_all x1, blocking collectives, body(): lax.all_to_all(both.reshape(group, piece, 128), ('wrap', 'x'), 0, 0, tile...  13.5 us
    ppermute x1, starting transfers between devices, body(): got_b = lax.ppermute(send_b, 'wrap', second)  6.08 us
    pallas_call x1, Pallas kernels, body(): call(lambda *refs: grad_kernel(rows, total, factor, *refs), (flat, edge,...  4.97 us
    ppermute x1, waiting for transfers between devices, body(): got_a = lax.ppermute(send_a, 'wrap', first)  4.87 us
    pallas_call x1, Pallas kernels, body(): call(lambda *refs: local_kernel(rows, *refs), (stack, stack, part, part,...  4.51 us
    unnamed x18, local copies, waits for them, and re-layouts  4.44 us
    all_to_all x1, starting transfers between devices, body(): lax.all_to_all(mine, ('wrap', 'x'), 0, 0, tiled=True).reshape(side, 128)  3.71 us
    ppermute x1, starting transfers between devices, body(): halo_b = lax.ppermute(hid_b, 'wrap', second)  3.29 us
  transfers between devices with their start and end apart: 7, of which 4 were waited for; matrix products, arithmetic and copies ran while one was open for 0% of the time, Pallas kernels for 18%

profile of v3, /device:TPU:0, one launch (start us, length us, event | category | flops | bytes accessed | tf_op | source)
XLA Modules:
  0.0 63.0 jit_solution(9168827257880335179)
XLA Ops:
  0.6 0.0 copy-start
  0.6 0.9 %copy-done = bf16[1,64,8,256]{3,2,1,0:T(8,128)(2,1)S(1)} copy-done((bf16[1,64,8,256]{3,2,1,0:T(8,128)(2,1)S(1)}, bf16[1,64,8,256]{3,2,1,0:T(8,128)(2,1)}, u32[]{:S(2)}) %copy-start) | copy-done | bytes 262168
  1.6 0.0 copy-start.1
  1.6 0.9 %copy-done.1 = bf16[1,64,8,256]{3,2,1,0:T(8,128)(2,1)S(1)} copy-done((bf16[1,64,8,256]{3,2,1,0:T(8,128)(2,1)S(1)}, bf16[1,64,8,256]{3,2,1,0:T(8,128)(2,1)}, u32[]{:S(2)}) %copy-start.1) | copy-done | bytes 262168
  2.5 1.1 %shard_map.110 = (bf16[512,256]{1,0:T(8,128)(2,1)S(1)}, bf16[512,256]{1,0:T(8,128)(2,1)S(1)}, bf16[512,256]{1,0:T(8,128)(2,1)S(1)}, bf16[512,256]{1,0:T(8,128)(2,1)S(1)}) custom-call(s32[1]{0:T(128)} %bitcast.refs_0_.refs_1_.refs_2_, s32[1]{0:T(128)} %bitcast.1.refs_1_.refs_0_, bf16[512,256]{1,0:T(8,128)(2,1)S(1)} %bitcast.14, bf16[512,256]{1,0:T(8,128)(2,1)S(1)} %bitcast.15), custom_call_target="tpu_custom_call" | custom-call | flops 100000000 | bytes 1000000 | tf_op jit(solution)/shard_map/pallas_call | solution.py:338
  3.7 6.1 %collective-permute-start = (bf16[512,256]{1,0:T(8,128)(2,1)S(1)}, bf16[512,256]{1,0:T(8,128)(2,1)S(1)}, u32[]{:S(2)}, u32[]{:S(2)}) collective-permute-start(bf16[512,256]{1,0:T(8,128)(2,1)S(1)} %get-tuple-element.32), channel_id=1, source_target_pairs={{0,28},{4,8},{8,4},{12,16},{16,12},{20,24},{24,20},{28,0},{1,29},{... | collective-permute-start | bytes 786440 | tf_op jit(solution)/shard_map/ppermute | solution.py:346
  9.8 0.0 collective-permute-start.1
  9.8 0.0 copy-start.2
  9.8 0.9 %copy-done.2 = bf16[64,1728]{1,0:T(8,128)(2,1)S(1)} copy-done((bf16[64,1728]{1,0:T(8,128)(2,1)S(1)}, bf16[64,1728]{1,0:T(8,128)(2,1)}, u32[]{:S(2)}) %copy-start.2) | copy-done | bytes 221208
  10.7 0.0 copy-start.3
  10.7 0.9 %copy-done.3 = bf16[64,1728]{1,0:T(8,128)(2,1)S(1)} copy-done((bf16[64,1728]{1,0:T(8,128)(2,1)S(1)}, bf16[64,1728]{1,0:T(8,128)(2,1)}, u32[]{:S(2)}) %copy-start.3) | copy-done | bytes 221208
  11.6 0.0 copy-start.6
  11.6 0.7 %copy-done.6 = s32[2]{0:T(128)S(1)} copy-done((s32[2]{0:T(128)S(1)}, s32[2]{0:T(128)}, u32[]{:S(2)}) %copy-start.6) | copy-done | bytes 32
  12.3 0.0 copy-start.7
  12.3 4.5 %shard_map.111 = (bf16[576,2048]{1,0:T(8,128)(2,1)S(1)}, bf16[576,2048]{1,0:T(8,128)(2,1)S(1)}, f32[64,2048]{1,0:T(8,128)S(1)}, f32[64,2048]{1,0:T(8,128)S(1)}, ...) custom-call(s32[2]{0:T(128)S(1)} %copy-done.6, ...), custom_call_target="tpu_custom_call" | custom-call | flops 4000000000 | bytes 8000000 | tf_op jit(solution)/shard_map/pallas_call | solution.py:352
  16.8 4.9 %collective-permute-done.1.refs_2_ = bf16[512,256]{1,0:T(8,128)(2,1)S(1)} collective-permute-done((bf16[512,256]{1,0:T(8,128)(2,1)S(1)}, bf16[512,256]{1,0:T(8,128)(2,1)S(1)}, u32[]{:S(2)}, u32[]{:S(2)}) %collective-permute-start.1) | collective-permute-done | bytes 262176 | tf_op jit(solution)/shard_map/ppermute | solution.py:345
  21.7 0.0 copy-done.7
  21.7 0.0 copy-start.5
  21.7 1.8 %shard_map.112 = (bf16[576,1024]{1,0:T(8,128)(2,1)S(1)}, bf16[576,1024]{1,0:T(8,128)(2,1)S(1)}, f32[64,2048]{1,0:T(8,128)S(1)}, f32[64,2048]{1,0:T(8,128)S(1)}) custom-call(s32[2]{0:T(128)S(1)} %copy-done.7, s32[1]{0:T(128)} %bitcast.refs_0_.refs_1_.refs_2_, bf16[512,256]{1,0:T(8,128)(2,1)S(1)} %collective-permute-done.1.refs_2_, ...), custom_call_target="tpu_custom_call" | custom-call | flops 2000000000 | bytes 4000000 | tf_op jit(solution)/shard_map/pallas_call | solution.py:368
  23.5 0.0 collective-permute-done.refs_4_
  23.5 0.0 copy-done.5
  23.5 5.0 %shard_map.113 = (bf16[512,256]{1,0:T(8,128)(2,1)S(1)}, bf16[256,256]{1,0:T(8,128)(2,1)S(1)}, bf16[256,256]{1,0:T(8,128)(2,1)S(1)}, f32[896,128]{1,0:T(8,128)S(1)}, bf16[896,128]{1,0:T(8,128)(2,1)S(1)}) custom-call(s32[2]{0:T(128)S(1)} %copy-done.7, s32[1]{0:T(128)} %bitcast.1.refs_1_.refs_0_, s32[1]{0:T(128)} %bitcast.refs_0_.refs_1_.refs_2_, ...), custom_call_target="tpu_custom_call" | custom-call | flops 4000000000 | bytes 8000000 | tf_op jit(solution)/shard_map/pallas_call | solution.py:379
  28.5 0.0 copy-start.4
  28.5 0.1 collective-permute-start.4
  28.6 1.5 %collective-permute-done.4.got_ref = bf16[896,128]{1,0:T(8,128)(2,1)S(1)} collective-permute-done((bf16[896,128]{1,0:T(8,128)(2,1)S(1)}, bf16[896,128]{1,0:T(8,128)(2,1)S(1)}, u32[]{:S(2)}, u32[]{:S(2)}) %collective-permute-start.4) | collective-permute-done | bytes 229408 | tf_op jit(solution)/shard_map/ppermute | solution.py:396
  30.1 13.5 %all_to_all.10.refs_0_ = bf16[16,56,128]{2,1,0:T(8,128)(2,1)S(1)} all-to-all(bf16[16,56,128]{2,1,0:T(8,128)(2,1)S(1)} %bitcast.11), channel_id=1, replica_groups=mesh['wrap'=8,'x'=2,'core'=2] {'wrap','x'}, dimensions={0} | all-to-all | bytes 458752 | tf_op jit(solution)/shard_map/all_to_all | solution.py:398
  43.6 0.7 %shard_map.117 = bf16[16,56,128]{2,1,0:T(8,128)(2,1)} custom-call(bf16[16,56,128]{2,1,0:T(8,128)(2,1)S(1)} %all_to_all.10.refs_0_), custom_call_target="tpu_custom_call" | custom-call | flops 100000000 | bytes 1000000 | tf_op jit(solution)/shard_map/pallas_call | solution.py:415
  44.3 3.7 %all-to-all-start.1 = ((bf16[16,56,128]{2,1,0:T(8,128)(2,1)}), bf16[16,56,128]{2,1,0:T(8,128)(2,1)S(1)}, u32[]{:S(2)}, u32[]{:S(2)}) async-start(bf16[16,56,128]{2,1,0:T(8,128)(2,1)} %shard_map.117), calls=%async_computation.1 | async-start | bytes 458752 | tf_op jit(solution)/shard_map/all_to_all | solution.py:416
  48.1 1.7 %collective-permute-start.2 = (bf16[256,256]{1,0:T(8,128)(2,1)S(1)}, bf16[256,256]{1,0:T(8,128)(2,1)S(1)}, u32[]{:S(2)}, u32[]{:S(2)}) collective-permute-start(bf16[256,256]{1,0:T(8,128)(2,1)S(1)} %get-tuple-element.48), channel_id=1, source_target_pairs={{0,4},{4,0},{8,12},{12,8},{16,20},{20,16},{24,28},{28,24},{1,5},{5... | collective-permute-start | bytes 393224 | tf_op jit(solution)/shard_map/ppermute | solution.py:399
  49.8 3.3 %collective-permute-start.3 = (bf16[256,256]{1,0:T(8,128)(2,1)S(1)}, bf16[256,256]{1,0:T(8,128)(2,1)S(1)}, u32[]{:S(2)}, u32[]{:S(2)}) collective-permute-start(bf16[256,256]{1,0:T(8,128)(2,1)S(1)} %get-tuple-element.49), channel_id=1, source_target_pairs={{0,28},{4,8},{8,4},{12,16},{16,12},{20,24},{24,20},{28,0},{1,29},{... | collective-permute-start | bytes 393224 | tf_op jit(solution)/shard_map/ppermute | solution.py:400
  53.1 0.0 copy-done.4
  53.1 0.0 copy-start.8
  53.1 2.3 %shard_map.114 = (f32[64,2048]{1,0:T(8,128)S(1)}, bf16[192,576]{1,0:T(8,128)(2,1)S(1)}) custom-call(s32[2]{0:T(128)S(1)} %copy-done.7, bf16[512,256]{1,0:T(8,128)(2,1)S(1)} %get-tuple-element.50.refs_1_, bf16[64,1728]{1,0:T(8,128)(2,1)S(1)} %copy-done.4, bf16[2304,256]{1,0:T(8,128)(2,1)S(1)} %get-tuple-element.41.refs_6_.refs_14_.refs_3_), custom_call_target="tpu_custom_call" | custom-call | flops 4000000000 | bytes 8000000 | tf_op jit(solution)/shard_map/pallas_call | solution.py:401
  55.4 2.7 %all-to-all-done.1 = bf16[16,56,128]{2,1,0:T(8,128)(2,1)S(1)} async-done(((bf16[16,56,128]{2,1,0:T(8,128)(2,1)}), bf16[16,56,128]{2,1,0:T(8,128)(2,1)S(1)}, u32[]{:S(2)}, u32[]{:S(2)}) %all-to-all-start.1) | async-done | bytes 229408 | tf_op jit(solution)/shard_map/all_to_all | solution.py:416
  58.1 0.0 collective-permute-start.5
  58.1 0.0 collective-permute-done.2.refs_2_
  58.1 0.8 %collective-permute-done.3.refs_3_ = bf16[256,256]{1,0:T(8,128)(2,1)S(1)} collective-permute-done((bf16[256,256]{1,0:T(8,128)(2,1)S(1)}, bf16[256,256]{1,0:T(8,128)(2,1)S(1)}, u32[]{:S(2)}, u32[]{:S(2)}) %collective-permute-start.3) | collective-permute-done | bytes 131104 | tf_op jit(solution)/shard_map/ppermute | solution.py:400
  58.9 0.0 copy-done.8
  58.9 2.9 %shard_map.115 = bf16[512,256]{1,0:T(8,128)(2,1)} custom-call(s32[2]{0:T(128)S(1)} %copy-done.7, s32[1]{0:T(128)} %bitcast.refs_0_.refs_1_.refs_2_, bf16[256,256]{1,0:T(8,128)(2,1)S(1)} %collective-permute-done.2.refs_2_, bf16[256,256]{1,0:T(8,128)(2,1)S(1)} %collective-permute-done.3.refs_3_, bf16[192,576]{1,0:T(8,128)(2,1)S(1)} %get-tuple-element.51.refs_4_, ...), custom_call_target="tpu_custom_call" | custom-call | flops 4000000000 | bytes 8000000 | tf_op jit(solution)/shard_map/pallas_call | solution.py:418
  61.9 0.0 collective-permute-done.5.refs_2_
  61.9 1.1 %shard_map.118 = (f32[64,1728]{1,0:T(8,128)}, f32[1,64]{1,0:T(1,128)}, f32[64,1728]{1,0:T(8,128)}, f32[1,64]{1,0:T(1,128)}) custom-call(s32[1]{0:T(128)} %bitcast.1.refs_1_.refs_0_, bf16[896,128]{1,0:T(8,128)(2,1)S(1)} %bitcast.13, bf16[896,128]{1,0:T(8,128)(2,1)S(1)} %collective-permute-done.5.refs_2_), custom_call_target="tpu_custom_call" | custom-call | flops 100000000 | bytes 1000000 | tf_op jit(solution)/shard_map/pallas_call | solution.py:433
  (1 shorter events, 0.0 us)
Async XLA Ops:
  0.6 1.0 %copy-start = (bf16[1,64,8,256]{3,2,1,0:T(8,128)(2,1)S(1)}, bf16[1,64,8,256]{3,2,1,0:T(8,128)(2,1)}, u32[]{:S(2)}) copy-start(bf16[1,64,8,256]{3,2,1,0:T(8,128)(2,1)} %param.7) | copy-start | bytes 786436
  1.6 0.9 %copy-start.1 = (bf16[1,64,8,256]{3,2,1,0:T(8,128)(2,1)S(1)}, bf16[1,64,8,256]{3,2,1,0:T(8,128)(2,1)}, u32[]{:S(2)}) copy-start(bf16[1,64,8,256]{3,2,1,0:T(8,128)(2,1)} %param.8) | copy-start | bytes 786436
  3.7 19.8 %collective-permute-start = (bf16[512,256]{1,0:T(8,128)(2,1)S(1)}, bf16[512,256]{1,0:T(8,128)(2,1)S(1)}, u32[]{:S(2)}, u32[]{:S(2)}) collective-permute-start(bf16[512,256]{1,0:T(8,128)(2,1)S(1)} %get-tuple-element.32), channel_id=1, source_target_pairs={{0,28},{4,8},{8,4},{12,16},{16,12},{20,24},{24,20},{28,0},{1,29},{... | collective-permute-start | bytes 786440 | tf_op jit(solution)/shard_map/ppermute | solution.py:346
  9.8 11.9 %collective-permute-start.1 = (bf16[512,256]{1,0:T(8,128)(2,1)S(1)}, bf16[512,256]{1,0:T(8,128)(2,1)S(1)}, u32[]{:S(2)}, u32[]{:S(2)}) collective-permute-start(bf16[512,256]{1,0:T(8,128)(2,1)S(1)} %get-tuple-element.39), channel_id=1, source_target_pairs={{0,4},{4,0},{8,12},{12,8},{16,20},{20,16},{24,28},{28,24},{1,5},{5... | collective-permute-start | bytes 786440 | tf_op jit(solution)/shard_map/ppermute | solution.py:345
  9.8 0.9 %copy-start.2 = (bf16[64,1728]{1,0:T(8,128)(2,1)S(1)}, bf16[64,1728]{1,0:T(8,128)(2,1)}, u32[]{:S(2)}) copy-start(bf16[64,1728]{1,0:T(8,128)(2,1)} %refs_3_.1) | copy-start | bytes 663556
  10.7 0.9 %copy-start.3 = (bf16[64,1728]{1,0:T(8,128)(2,1)S(1)}, bf16[64,1728]{1,0:T(8,128)(2,1)}, u32[]{:S(2)}) copy-start(bf16[64,1728]{1,0:T(8,128)(2,1)} %refs_2_.1) | copy-start | bytes 663556
  11.6 0.7 %copy-start.6 = (s32[2]{0:T(128)S(1)}, s32[2]{0:T(128)}, u32[]{:S(2)}) copy-start(s32[2]{0:T(128)} %refs_0_.9) | copy-start | bytes 28
  12.3 9.4 %copy-start.7 = (s32[2]{0:T(128)S(1)}, s32[2]{0:T(128)}, u32[]{:S(2)}) copy-start(s32[2]{0:T(128)} %refs_0_.9) | copy-start | bytes 28
  21.7 1.8 %copy-start.5 = (f32[64]{0:T(128)S(1)}, f32[64]{0:T(128)}, u32[]{:S(2)}) copy-start(f32[64]{0:T(128)} %param.10) | copy-start | bytes 772
  28.5 24.6 %copy-start.4 = (bf16[64,1728]{1,0:T(8,128)(2,1)S(1)}, bf16[64,1728]{1,0:T(8,128)(2,1)}, u32[]{:S(2)}) copy-start(bf16[64,1728]{1,0:T(8,128)(2,1)} %refs_2_.1) | copy-start | bytes 663556
  28.5 1.6 %collective-permute-start.4 = (bf16[896,128]{1,0:T(8,128)(2,1)S(1)}, bf16[896,128]{1,0:T(8,128)(2,1)S(1)}, u32[]{:S(2)}, u32[]{:S(2)}) collective-permute-start(bf16[896,128]{1,0:T(8,128)(2,1)S(1)} %get-tuple-element.54), channel_id=1, source_target_pairs={{0,1},{1,0},{2,3},{3,2},{4,5},{5,4},{6,7},{7,6},{8,9},{9,8},{10,11... | collective-permute-start | bytes 688136 | tf_op jit(solution)/shard_map/ppermute | solution.py:396
  44.3 13.8 %all-to-all-start.1 = ((bf16[16,56,128]{2,1,0:T(8,128)(2,1)}), bf16[16,56,128]{2,1,0:T(8,128)(2,1)S(1)}, u32[]{:S(2)}, u32[]{:S(2)}) async-start(bf16[16,56,128]{2,1,0:T(8,128)(2,1)} %shard_map.117), calls=%async_computation.1 | async-start | bytes 458752 | tf_op jit(solution)/shard_map/all_to_all | solution.py:416
  48.1 10.1 %collective-permute-start.2 = (bf16[256,256]{1,0:T(8,128)(2,1)S(1)}, bf16[256,256]{1,0:T(8,128)(2,1)S(1)}, u32[]{:S(2)}, u32[]{:S(2)}) collective-permute-start(bf16[256,256]{1,0:T(8,128)(2,1)S(1)} %get-tuple-element.48), channel_id=1, source_target_pairs={{0,4},{4,0},{8,12},{12,8},{16,20},{20,16},{24,28},{28,24},{1,5},{5... | collective-permute-start | bytes 393224 | tf_op jit(solution)/shard_map/ppermute | solution.py:399
  49.8 9.1 %collective-permute-start.3 = (bf16[256,256]{1,0:T(8,128)(2,1)S(1)}, bf16[256,256]{1,0:T(8,128)(2,1)S(1)}, u32[]{:S(2)}, u32[]{:S(2)}) collective-permute-start(bf16[256,256]{1,0:T(8,128)(2,1)S(1)} %get-tuple-element.49), channel_id=1, source_target_pairs={{0,28},{4,8},{8,4},{12,16},{16,12},{20,24},{24,20},{28,0},{1,29},{... | collective-permute-start | bytes 393224 | tf_op jit(solution)/shard_map/ppermute | solution.py:400
  53.1 5.8 %copy-start.8 = (f32[64]{0:T(128)S(1)}, f32[64]{0:T(128)}, u32[]{:S(2)}) copy-start(f32[64]{0:T(128)} %param.12) | copy-start | bytes 772
  58.1 3.7 %collective-permute-start.5 = (bf16[896,128]{1,0:T(8,128)(2,1)S(1)}, bf16[896,128]{1,0:T(8,128)(2,1)S(1)}, u32[]{:S(2)}, u32[]{:S(2)}) collective-permute-start(bf16[896,128]{1,0:T(8,128)(2,1)S(1)} %bitcast.12), channel_id=1, source_target_pairs={{0,1},{1,0},{2,3},{3,2},{4,5},{5,4},{6,7},{7,6},{8,9},{9,8},{10,11... | collective-permute-start | bytes 688136 | tf_op jit(solution)/shard_map/ppermute | solution.py:417
